TPU v7x, 512 devices: a whole 4x8x8 slice. The times are simulated.
512 devices in a mesh: tile: 128 (over z, y_lo, x, core), comp: 4 (over y_hi).
Axes of the slice: x: 4, y: 8 (y_hi: 4, y_lo: 2; y = y_hi * 2 + y_lo), z: 8, core: 2. Of those that a mesh axis runs over, the one named last changes fastest.
Arguments:
- species_concentration: float32 [48, 88, 512, 128], P('comp', None, 'tile'), may hold values from 0.05 to 2
- courant_face_numbers: float32 [2, 88, 512, 128], P(None, 'comp', 'tile'), may hold values from -0.24 to 0.24
- diffusive_interface_factor: float32 [88, 512, 128], P('comp', 'tile'), may hold values from 0.05 to 3
- thermal_anomaly_field: float32 [88, 512, 128], P('comp', 'tile'), may hold values from -6 to 6
- seawater_indicator: int32 [512, 128], P('tile'), may hold values 0 or 1
- wet_layer_number: int32 [512, 128], P('tile'), may hold values from 1 to 88
- species_coupling_matrix: float32 [48, 48], replicated, may hold values from -0.875 to 0.875
- species_photic_factor: float32 [48], replicated, may hold values from -2 to 2
- species_loss_factor: float32 [48], replicated, may hold values from 0.2 to 2
Outputs:
- updated_species_field: float32 [48, 88, 512, 128], P('comp', None, 'tile')
- temperature_out: float32 [88, 512, 128], P('comp', 'tile')
All inputs are finite; a program needn't handle non-finite values. No bound on the sum of `seawater_indicator` on one device may be relied on, other than what follows from the above.
Results may differ from a plain program's by a relative error of at most 0.0001.
Values sent between devices are 32-bit elements; how exact they have to be, the bound alone decides.
No kernel may reach another device: no remote copies, remote signals or barrier semaphores. Data moves between devices by JAX's collectives and lax.ppermute only.
A program may use at most 64 MiB of HBM per device.

v0:
```python
import jax
import jax.numpy as jnp
from jax import lax
from jax.sharding import PartitionSpec as P

ADVECT = 2
SUBSTEPS = 4


RATE_STEP = 0.25
HEAT_GAIN = 2.0


def padded(block, sides, width):
    for axis, dim in sides:
        count = lax.axis_size(axis)
        forward = [(i, i + 1) for i in range(count - 1)]
        backward = [(target, source) for source, target in forward]
        low = lax.ppermute(
            lax.slice_in_dim(block, block.shape[dim] - width, None, axis=dim), axis, forward
        )
        high = lax.ppermute(lax.slice_in_dim(block, 0, width, axis=dim), axis, backward)
        block = jnp.concatenate([low, block, high], axis=dim)
    return block


def copy_for_each(x, axis):
    copies = jnp.broadcast_to(x, (lax.axis_size(axis), *x.shape))
    return lax.all_to_all(copies, axis, split_axis=0, concat_axis=0, tiled=True)


def joined_by_halves(pieces, combine):
    while len(jax.tree.leaves(pieces)[0]) > 1:
        pieces = jax.vmap(combine)(*(pieces[side::2] for side in (0, 1)))
    return pieces[0]


def prefix(x, axis, combine, identity):
    peers, index = (lax.axis_size(axis), lax.axis_index(axis))
    passed = jnp.arange(peers) < index

    def kept(part, zero, own):
        part = jnp.where(
            passed.reshape(-1, *(1 for _ in own.shape)), part, jnp.asarray(zero, own.dtype)
        )
        return part

    pieces = copy_for_each(x, axis)
    return joined_by_halves(kept(pieces, identity, x), combine)


def activity(seawater_indicator, wet_layer_number, first_level, count):
    level_index = first_level + jnp.arange(count, dtype=jnp.int32)
    inside = (level_index[:, None, None] < wet_layer_number[None]) & (seawater_indicator[None] > 0)
    return inside.astype(jnp.float32)


def advance(conc, active, east, north):
    open_east = active[:, :-1] * active[:, 1:]
    speed_east = east[:, :-1] * open_east
    flux_east = (
        jnp.maximum(speed_east, 0.0) * conc[:, :, :-1]
        + jnp.minimum(speed_east, 0.0) * conc[:, :, 1:]
    )
    inner = conc[:, :, 1:-1]
    active_inner = active[:, 1:-1]
    open_north = active_inner[:, :, :-1] * active_inner[:, :, 1:]
    speed_north = north[:, 1:-1, :-1] * open_north
    flux_north = (
        jnp.maximum(speed_north, 0.0) * inner[..., :-1]
        + jnp.minimum(speed_north, 0.0) * inner[..., 1:]
    )
    flux_north = jnp.pad(flux_north, ((0, 0), (0, 0), (0, 0), (1, 1)))
    return (
        inner
        - (flux_east[:, :, 1:] - flux_east[:, :, :-1])
        - (flux_north[..., 1:] - flux_north[..., :-1])
    )


def diffuse(conc, diffusive_interface_factor, active):
    levels = conc.shape[1]
    coupling = diffusive_interface_factor[:-1] * active[:-1] * active[1:]
    nothing = jnp.zeros_like(diffusive_interface_factor[0])
    ratios = []
    partial_list = []
    for level in range(levels):
        coupling_up = coupling[level - 1] if level > 0 else nothing
        coupling_down = coupling[level] if level < levels - 1 else nothing
        pivot = 1.0 + coupling_up + coupling_down
        source = conc[:, level]
        if level > 0:
            pivot = pivot + coupling_up * ratios[-1]
            source = source + coupling_up * partial_list[-1]
        ratios.append(-coupling_down / pivot)
        partial_list.append(source / pivot)
    solved = [partial_list[-1]]
    for level in range(levels - 2, -1, -1):
        solved.append(partial_list[level] - ratios[level] * solved[-1])
    solved = solved[::-1]
    return jnp.stack(solved, axis=1)


def reaction(
    conc, light_level, active, species_coupling_matrix, species_photic_factor, species_loss_factor
):
    layout_shape = conc.shape
    columns_flat = conc.reshape(layout_shape[0], -1)
    light_flat = light_level.reshape(1, -1)
    active_flat = active.reshape(1, -1)
    for substep in range(SUBSTEPS):
        forcing = jnp.dot(
            species_coupling_matrix,
            columns_flat,
            precision=lax.Precision.HIGHEST,
            preferred_element_type=jnp.float32,
        )
        forcing = forcing + species_photic_factor[:, None] * light_flat
        columns_flat = columns_flat + RATE_STEP * active_flat * (
            jnp.tanh(forcing) - species_loss_factor[:, None] * columns_flat
        )
    return columns_flat.reshape(layout_shape)


def add_depth(earlier, later):
    return earlier + later


def body(
    species_concentration,
    courant_face_numbers,
    diffusive_interface_factor,
    thermal_anomaly_field,
    seawater_indicator,
    wet_layer_number,
    species_coupling_matrix,
    species_photic_factor,
    species_loss_factor,
):
    velocity_all, mixing_all = (
        lax.all_gather(courant_face_numbers, "comp", axis=1, tiled=True),
        lax.all_gather(diffusive_interface_factor, "comp", axis=0, tiled=True),
    )
    levels_total = mixing_all.shape[0]
    active = activity(seawater_indicator, wet_layer_number, 0, levels_total)
    groups = species_concentration.shape[0]
    stacked = jnp.concatenate([species_concentration, active[None], velocity_all], axis=0)
    current = species_concentration
    for advect_step in range(ADVECT):
        layered = jnp.concatenate([current, stacked[groups:]], axis=0)
        extended = padded(layered, (("tile", 2),), 1)
        current = advance(
            extended[:groups], extended[groups], extended[groups + 1], extended[groups + 2]
        )
    diffused = diffuse(current, mixing_all, active)
    comp_index = lax.axis_index("comp")
    gathered = lax.all_to_all(diffused, "comp", split_axis=1, concat_axis=0, tiled=True)
    level_share = gathered.shape[1]
    active_share = activity(
        seawater_indicator, wet_layer_number, comp_index * level_share, level_share
    )
    attenuation = 0.05 + 0.1 * gathered[0]
    running = jnp.cumsum(attenuation, axis=0)
    depth_offset = prefix(running[-1], "comp", add_depth, jnp.zeros_like(running[-1]))
    light_level = jnp.exp(-(depth_offset[None] + running - attenuation))
    reacted = reaction(
        gathered,
        light_level,
        active_share,
        species_coupling_matrix,
        species_photic_factor,
        species_loss_factor,
    )
    updated_species_field = lax.all_to_all(reacted, "comp", split_axis=0, concat_axis=1, tiled=True)
    sunlight_warming = HEAT_GAIN * active_share * light_level * (1.0 - jnp.exp(-attenuation))
    return (updated_species_field, thermal_anomaly_field + sunlight_warming)


def solution(mesh):
    in_specs = (
        P("comp", None, "tile", None),
        P(None, "comp", "tile", None),
        P("comp", "tile", None),
        P("comp", "tile", None),
        P("tile", None),
        P("tile", None),
        P(),
        P(),
        P(),
    )
    out_specs = (P("comp", None, "tile", None), P("comp", "tile", None))
    return jax.shard_map(body, mesh=mesh, in_specs=in_specs, out_specs=out_specs, check_vma=False)
```

profile of v0, /device:TPU:6, one launch (start us, length us, event | category | flops | bytes accessed | tf_op | source)
XLA Modules:
  0.0 218.8 jit_solution(3037064828222277415)
XLA Ops:
  2.2 17.5 %all_gather.6 = f32[2,88,4,128]{3,2,0,1:T(4,128)S(1)} all-gather(f32[2,22,4,128]{3,2,0,1:T(4,128)S(1)} %copy.866), channel_id=1, replica_groups=mesh['tile'=128,'comp'=4] {'comp'}, dimensions={1}, use_global_device_ids=true | all-gather | bytes 450560 | tf_op jit(solution)/shard_map/all_gather | solution.py:141
  20.0 2.9 %copy.879 = f32[12,88,4,128]{3,0,2,1:T(8,128)S(1)} copy(f32[12,88,4,128]{3,2,1,0:T(4,128)} %param.9) | data formatting | bytes 4325376 | tf_op args[0]
  24.0 1.9 collective-permute-start.1
  26.2 2.4 %collective-permute-start = (f32[15,88,1,128]{3,1,2,0:T(8,128)S(1)}, f32[15,88,1,128]{3,1,2,0:T(8,128)S(1)}, u32[]{:S(2)}, u32[]{:S(2)}) collective-permute-start(f32[15,88,1,128]{3,1,2,0:T(8,128)S(1)} %copy.869), channel_id=1, source_target_pairs={{0,4},{4,8},{8,12},{12,16},{16,20},{20,24},{24,28},{28,32},{32,36}... | collective-permute-start | bytes 2027528 | tf_op jit(solution)/shard_map/ppermute | solution.py:19
  28.7 14.2 %all_gather.7 = f32[88,4,128]{2,1,0:T(4,128)S(1)} all-gather(f32[22,4,128]{2,1,0:T(4,128)S(1)} %copy-done.3), channel_id=1, replica_groups=mesh['tile'=128,'comp'=4] {'comp'}, dimensions={0}, use_global_device_ids=true | all-gather | bytes 225280 | tf_op jit(solution)/shard_map/all_gather | solution.py:142
  49.2 2.2 fusion.35
  52.6 1.9 collective-permute-start.3
  54.5 5.2 %collective-permute-start.2 = (f32[15,88,1,128]{3,1,2,0:T(8,128)S(1)}, f32[15,88,1,128]{3,1,2,0:T(8,128)S(1)}, u32[]{:S(2)}, u32[]{:S(2)}) collective-permute-start(f32[15,88,1,128]{3,1,2,0:T(8,128)S(1)} %copy.886), channel_id=1, source_target_pairs={{0,4},{4,8},{8,12},{12,16},{16,20},{20,24},{24,28},{28,32},{32,36}... | collective-permute-start | bytes 2027528 | tf_op jit(solution)/shard_map/ppermute | solution.py:19
  60.6 2.2 %collective-permute-done.3 = f32[15,88,1,128]{3,1,2,0:T(8,128)S(1)} collective-permute-done((f32[15,88,1,128]{3,1,2,0:T(8,128)S(1)}, f32[15,88,1,128]{3,1,2,0:T(8,128)S(1)}, u32[]{:S(2)}, u32[]{:S(2)}) %collective-permute-start.3) | collective-permute-done | bytes 675872 | tf_op jit(solution)/shard_map/ppermute | solution.py:22
  63.0 3.7 %collective-permute-done.2 = f32[15,88,1,128]{3,1,2,0:T(8,128)S(1)} collective-permute-done((f32[15,88,1,128]{3,1,2,0:T(8,128)S(1)}, f32[15,88,1,128]{3,1,2,0:T(8,128)S(1)}, u32[]{:S(2)}, u32[]{:S(2)}) %collective-permute-start.2) | collective-permute-done | bytes 675872 | tf_op jit(solution)/shard_map/ppermute | solution.py:19
  73.2 3.2 %constant_dynamic-update-slice_fusion.87 = (f32[12,88,4,128]{3,0,2,1:T(8,128)S(1)}, f32[12,4,128]{2,0,1:T(8,128)S(1)}, f32[12,4,128]{2,0,1:T(8,128)S(1)}, f32[12...) fusion(f32[4,128]{1,0:T(4,128)S(1)} %get-tuple-element.269, ...), kind=kLoop, calls=%fused_computation.170 | loop fusion | flops 2365439 | bytes 4497408
  79.4 2.4 %copy.899 = f32[12,88,4,128]{3,2,0,1:T(4,128)} copy(f32[12,88,4,128]{3,0,2,1:T(8,128)S(1)} %constant_dynamic-update-slice_fusion) | data formatting | bytes 4325376 | tf_op jit(solution)/shard_map/stack | solution.py:101
  81.8 4.7 %all-to-all-start = ((f32[12,88,4,128]{3,2,0,1:T(4,128)}), f32[12,88,4,128]{3,2,0,1:T(4,128)S(1)}, u32[]{:S(2)}, u32[]{:S(2)}) async-start(f32[12,88,4,128]{3,2,0,1:T(4,128)} %copy.899), calls=%async_computation | async-start | bytes 4325376 | tf_op jit(solution)/shard_map/all_to_all | solution.py:157
  86.5 50.4 %all-to-all-done = f32[12,88,4,128]{3,2,0,1:T(4,128)S(1)} async-done(((f32[12,88,4,128]{3,2,0,1:T(4,128)}), f32[12,88,4,128]{3,2,0,1:T(4,128)S(1)}, u32[]{:S(2)}, u32[]{:S(2)}) %all-to-all-start) | async-done | bytes 2162720 | tf_op jit(solution)/shard_map/all_to_all | solution.py:157
  138.2 2.0 copy.915
  140.9 4.4 %all-to-all-start.1 = ((f32[4,4,128]{2,1,0:T(4,128)}), f32[4,4,128]{2,1,0:T(4,128)S(1)}, u32[]{:S(2)}, u32[]{:S(2)}) async-start(f32[4,4,128]{2,1,0:T(4,128)} %broadcast_in_dim.11), calls=%async_computation.1 | async-start | bytes 16384 | tf_op jit(solution)/shard_map/all_to_all | solution.py:29
  145.3 2.0 reshape.190
  147.3 5.7 %all-to-all-done.1 = f32[4,4,128]{2,1,0:T(4,128)S(1)} async-done(((f32[4,4,128]{2,1,0:T(4,128)}), f32[4,4,128]{2,1,0:T(4,128)S(1)}, u32[]{:S(2)}, u32[]{:S(2)}) %all-to-all-start.1) | async-done | bytes 8224 | tf_op jit(solution)/shard_map/all_to_all | solution.py:29
  153.9 4.7 %fusion.19 = f32[48,11264]{1,0:T(8,128)S(1)} fusion(f32[48,11264]{1,0:T(8,128)} %reshape.190, f32[48,48]{1,0:T(8,128)S(1)} %copy-done, f32[48]{0:T(128)S(1)} %copy-done.6, f32[11264]{0:T(1024)S(1)} %negate_exponential_fusion, f32[48]{0:T(128)S(1)} %copy-done.7, f32[11264]{0:T(1024)S(1)} %bitcast.1781), kind=kOutput, calls=%fused_computation.23 | convolution fusion | flops 314671104 | bytes 4425088 | tf_op jit(solution)/shard_map/dot_general | solution.py:112
  158.6 2.5 %fusion.14 = f32[48,11264]{1,0:T(8,128)S(1)} fusion(f32[48,11264]{1,0:T(8,128)S(1)} %fusion.19, f32[48,48]{1,0:T(8,128)S(1)} %copy-done, f32[48]{0:T(128)S(1)} %copy-done.6, f32[11264]{0:T(1024)S(1)} %negate_exponential_fusion, f32[48]{0:T(128)S(1)} %copy-done.7, f32[11264]{0:T(1024)S(1)} %bitcast.1782), kind=kOutput, calls=%fused_computation.17 | convolution fusion | flops 314671104 | bytes 4425088 | tf_op jit(solution)/shard_map/dot_general | solution.py:112
  161.0 2.4 %fusion.9 = f32[48,11264]{1,0:T(8,128)S(1)} fusion(f32[48,11264]{1,0:T(8,128)S(1)} %fusion.14, f32[48,48]{1,0:T(8,128)S(1)} %copy-done, f32[48]{0:T(128)S(1)} %copy-done.6, f32[11264]{0:T(1024)S(1)} %negate_exponential_fusion, f32[48]{0:T(128)S(1)} %copy-done.7, f32[11264]{0:T(1024)S(1)} %bitcast.1783), kind=kOutput, calls=%fused_computation.11 | convolution fusion | flops 314671104 | bytes 4425088 | tf_op jit(solution)/shard_map/dot_general | solution.py:112
  163.5 3.8 %fusion.4 = f32[48,11264]{1,0:T(8,128)} fusion(f32[48,11264]{1,0:T(8,128)S(1)} %fusion.9, f32[48,48]{1,0:T(8,128)S(1)} %copy-done, f32[48]{0:T(128)S(1)} %copy-done.6, f32[11264]{0:T(1024)S(1)} %negate_exponential_fusion, f32[48]{0:T(128)S(1)} %copy-done.7, f32[11264]{0:T(1024)S(1)} %bitcast.1784), kind=kOutput, calls=%fused_computation.5 | convolution fusion | flops 314671104 | bytes 4425088 | tf_op jit(solution)/shard_map/dot_general | solution.py:112
  167.3 2.2 %reshape.191 = f32[48,22,4,128]{3,2,1,0:T(4,128)S(1)} reshape(f32[48,11264]{1,0:T(8,128)} %fusion.4) | data formatting | bytes 4325376 | tf_op jit(solution)/shard_map/reshape | solution.py:122
  169.5 47.7 %all_to_all.41 = f32[48,22,4,128]{3,2,1,0:T(4,128)S(1)} all-to-all(f32[48,22,4,128]{3,2,1,0:T(4,128)S(1)} %reshape.191), channel_id=1, replica_groups=mesh['tile'=128,'comp'=4] {'comp'}, dimensions={0} | all-to-all | bytes 4325376 | tf_op jit(solution)/shard_map/all_to_all | solution.py:174
  (177 shorter events, 24.6 us)
Async XLA Ops:
  0.6 153.2 %copy-start = (f32[48,48]{1,0:T(8,128)S(1)}, f32[48,48]{1,0:T(8,128)}, u32[]{:S(2)}) copy-start(f32[48,48]{1,0:T(8,128)} %param.15) | copy-start | bytes 27652
  19.8 3.1 %copy-start.5 = (s32[4,128]{1,0:T(4,128)S(1)}, s32[4,128]{1,0:T(4,128)}, u32[]{:S(2)}) copy-start(s32[4,128]{1,0:T(4,128)} %param.14) | copy-start | bytes 6148
  23.7 5.0 %copy-start.3 = (f32[22,4,128]{2,1,0:T(4,128)S(1)}, f32[22,4,128]{2,1,0:T(4,128)}, u32[]{:S(2)}) copy-start(f32[22,4,128]{2,1,0:T(4,128)} %param.11) | copy-start | bytes 135172
  24.0 19.6 %collective-permute-start.1 = (f32[15,88,1,128]{3,1,2,0:T(8,128)S(1)}, f32[15,88,1,128]{3,1,2,0:T(8,128)S(1)}, u32[]{:S(2)}, u32[]{:S(2)}) collective-permute-start(f32[15,88,1,128]{3,1,2,0:T(8,128)S(1)} %copy.870), channel_id=1, source_target_pairs={{4,0},{8,4},{12,8},{16,12},{20,16},{24,20},{28,24},{32,28},{36,32}... | collective-permute-start | bytes 2027528 | tf_op jit(solution)/shard_map/ppermute | solution.py:22
  26.2 17.6 %collective-permute-start = (f32[15,88,1,128]{3,1,2,0:T(8,128)S(1)}, f32[15,88,1,128]{3,1,2,0:T(8,128)S(1)}, u32[]{:S(2)}, u32[]{:S(2)}) collective-permute-start(f32[15,88,1,128]{3,1,2,0:T(8,128)S(1)} %copy.869), channel_id=1, source_target_pairs={{0,4},{4,8},{8,12},{12,16},{16,20},{20,24},{24,28},{28,32},{32,36}... | collective-permute-start | bytes 2027528 | tf_op jit(solution)/shard_map/ppermute | solution.py:19
  47.6 1.6 copy-start.1
  52.6 10.2 %collective-permute-start.3 = (f32[15,88,1,128]{3,1,2,0:T(8,128)S(1)}, f32[15,88,1,128]{3,1,2,0:T(8,128)S(1)}, u32[]{:S(2)}, u32[]{:S(2)}) collective-permute-start(f32[15,88,1,128]{3,1,2,0:T(8,128)S(1)} %copy.887), channel_id=1, source_target_pairs={{4,0},{8,4},{12,8},{16,12},{20,16},{24,20},{28,24},{32,28},{36,32}... | collective-permute-start | bytes 2027528 | tf_op jit(solution)/shard_map/ppermute | solution.py:22
  54.5 12.1 %collective-permute-start.2 = (f32[15,88,1,128]{3,1,2,0:T(8,128)S(1)}, f32[15,88,1,128]{3,1,2,0:T(8,128)S(1)}, u32[]{:S(2)}, u32[]{:S(2)}) collective-permute-start(f32[15,88,1,128]{3,1,2,0:T(8,128)S(1)} %copy.886), channel_id=1, source_target_pairs={{0,4},{4,8},{8,12},{12,16},{16,20},{20,24},{24,28},{28,32},{32,36}... | collective-permute-start | bytes 2027528 | tf_op jit(solution)/shard_map/ppermute | solution.py:19
  81.8 55.1 %all-to-all-start = ((f32[12,88,4,128]{3,2,0,1:T(4,128)}), f32[12,88,4,128]{3,2,0,1:T(4,128)S(1)}, u32[]{:S(2)}, u32[]{:S(2)}) async-start(f32[12,88,4,128]{3,2,0,1:T(4,128)} %copy.899), calls=%async_computation | async-start | bytes 4325376 | tf_op jit(solution)/shard_map/all_to_all | solution.py:157
  136.9 1.3 copy-start.2
  140.2 12.9 %copy-start.4 = (f32[22,4,128]{2,1,0:T(4,128)S(1)}, f32[22,4,128]{2,1,0:T(4,128)}, u32[]{:S(2)}) copy-start(f32[22,4,128]{2,1,0:T(4,128)} %param.12) | copy-start | bytes 135172
  140.2 13.7 %copy-start.6 = (f32[48]{0:T(128)S(1)}, f32[48]{0:T(128)}, u32[]{:S(2)}) copy-start(f32[48]{0:T(128)} %param.17) | copy-start | bytes 580
  140.2 13.7 %copy-start.7 = (f32[48]{0:T(128)S(1)}, f32[48]{0:T(128)}, u32[]{:S(2)}) copy-start(f32[48]{0:T(128)} %param.16) | copy-start | bytes 580
  140.9 12.2 %all-to-all-start.1 = ((f32[4,4,128]{2,1,0:T(4,128)}), f32[4,4,128]{2,1,0:T(4,128)S(1)}, u32[]{:S(2)}, u32[]{:S(2)}) async-start(f32[4,4,128]{2,1,0:T(4,128)} %broadcast_in_dim.11), calls=%async_computation.1 | async-start | bytes 16384 | tf_op jit(solution)/shard_map/all_to_all | solution.py:29
where the time goes:
time: 220 us; the launch traced here: 219 us
  blocking collectives  79.5 us (36%)
  waiting for transfers between devices  62 us (28%)
  local copies, waits for them, and re-layouts  20.7 us (9%)
  other arithmetic  20.7 us (9%)
  starting transfers between devices  20.6 us (9%)
  matrix products  13.4 us (6%)
    all_to_all x1, waiting for transfers between devices, body(): lax.all_to_all(diffused, 'comp', split_axis=1, concat_axis=0, tiled=True)  50.4 us
    all_to_all x1, blocking collectives, body(): lax.all_to_all(reacted, 'comp', split_axis=0, concat_axis=1, tiled=True)  47.7 us
    all_gather x1, blocking collectives, body(): lax.all_gather(courant_face_numbers, 'comp', axis=1, tiled=True)  17.5 us
    all_gather x1, blocking collectives, body(): lax.all_gather(diffusive_interface_factor, 'comp', axis=0, tiled=True)  14.2 us
    dot_general x4, matrix products, reaction(): jnp.dot(species_coupling_matrix, columns_flat, precision=lax.Precision.HI...  13.4 us
    ppermute x2, starting transfers between devices, padded(): lax.ppermute(lax.slice_in_dim(block, block.shape[dim] - width, None, axis...  7.61 us
    unnamed x61, local copies, waits for them, and re-layouts  6.21 us
    all_to_all x1, waiting for transfers between devices, copy_for_each(): return lax.all_to_all(copies, axis, split_axis=0, concat_axis=0, tiled=True)  5.74 us
  transfers between devices with their start and end apart: 6, of which 4 were waited for; matrix products, arithmetic and copies ran while one was open for 2% of the time, Pallas kernels for 0%

commit v1 on v0

v1 whole, which is shorter than its diff:
```python
import jax
import jax.numpy as jnp
from jax import lax
from jax.experimental import pallas as pl
from jax.experimental.pallas import tpu as pltpu
from jax.sharding import PartitionSpec as P

ADVECT = 2
SUBSTEPS = 4
RATE_STEP = 0.25
HEAT_GAIN = 2.0
LANES = 128
HALO = 2
ROWS = 8
F32 = jnp.float32
BF16 = jnp.bfloat16
VMEM = pl.BlockSpec(memory_space=pltpu.VMEM)
SMEM = pl.BlockSpec(memory_space=pltpu.SMEM)


def call(kernel, outs, scratch=(), ins=None, mib=24):
    return pl.pallas_call(
        kernel,
        out_shape=outs,
        in_specs=ins,
        out_specs=jax.tree.map(lambda _: VMEM, outs),
        scratch_shapes=list(scratch),
        compiler_params=pltpu.CompilerParams(vmem_limit_bytes=mib << 20),
    )


def iota(shape, dim):
    return lax.broadcasted_iota(jnp.int32, shape, dim)


def split3(x):
    hi = x.astype(BF16)
    rest = x - hi.astype(F32)
    mid = rest.astype(BF16)
    low = (rest - mid.astype(F32)).astype(BF16)
    return hi, mid, low


def picked(x, onehot):
    total = None
    for part in split3(x):
        term = jnp.dot(part, onehot, preferred_element_type=F32)
        total = term if total is None else total + term
    return total


def pairing_kernel(levels, depth_ref, fold_ref, unfold_ref, rank_ref, lane_ref):
    width = depth_ref.shape[0]
    columns = width * LANES
    lanes = columns // 2
    depth = depth_ref[...]
    wide = jnp.concatenate([depth] * (LANES // width), axis=0)
    upright = wide.T
    a = jnp.zeros((1, lanes), F32)
    b = jnp.zeros((1, lanes), F32)
    rank_ref[...] = jnp.zeros_like(rank_ref)
    for i in range(width):
        own_col = upright[:, i : i + 1]
        own_row = depth[i : i + 1, :]
        rank_col = jnp.zeros((LANES, 1), F32)
        rank_row = jnp.zeros((1, LANES), F32)
        mine_col = i * LANES + iota((LANES, LANES), 0)
        mine_row = i * LANES + iota((LANES, LANES), 1)
        for o in range(width):
            other_row = depth[o : o + 1, :]
            other_col = upright[:, o : o + 1]
            index_row = o * LANES + iota((LANES, LANES), 1)
            index_col = o * LANES + iota((LANES, LANES), 0)
            ahead = (other_row > own_col) | ((other_row == own_col) & (index_row < mine_col))
            rank_col = rank_col + jnp.sum(jnp.where(ahead, 1.0, 0.0), axis=1, keepdims=True)
            ahead = (other_col > own_row) | ((other_col == own_row) & (index_col < mine_row))
            rank_row = rank_row + jnp.sum(jnp.where(ahead, 1.0, 0.0), axis=0, keepdims=True)
        half = float(lanes)
        last = float(columns - 1)
        lane_col = jnp.where(rank_col < half, rank_col, last - rank_col)
        hit = lane_col == iota((LANES, lanes), 1).astype(F32)
        fold_ref[i] = jnp.where(hit, 1.0, 0.0).astype(BF16)
        deep = hit & (rank_col < half)
        a = a + jnp.sum(jnp.where(deep, own_col, 0.0), axis=0, keepdims=True)
        b = b + jnp.sum(jnp.where(hit & (rank_col >= half), own_col, 0.0), axis=0, keepdims=True)
        lane_row = jnp.where(rank_row < half, rank_row, last - rank_row)
        unfold_ref[:, i * LANES : (i + 1) * LANES] = jnp.where(
            lane_row == iota((lanes, LANES), 0).astype(F32), 1.0, 0.0
        ).astype(BF16)
        rank_ref[i : i + 1, :] = rank_row
    lane_ref[...] = jnp.zeros_like(lane_ref)
    lane_ref[0:1, :] = a
    lane_ref[1:2, :] = b
    over = jnp.max(jnp.where(a + b > float(levels), 1.0, 0.0), axis=1, keepdims=True)
    lane_ref[2:3, :] = jnp.broadcast_to(over, (1, lanes))


def pack(deep, shallow, x_ref, fold_ref, out_ref, depth, levels, groups):
    pass


def transport_kernel(
    c_ref, face_ref, depth_ref, side_ref, fold_ref, out_ref, x_ref, ratio_ref
):
    groups, levels = c_ref.shape[:2]
    half = levels // 2
    depth = depth_ref[...]
    row = iota((ROWS, LANES), 0)
    lane = iota((ROWS, LANES), 1)
    inner_east = row < ROWS - 1
    inner_north = lane < LANES - 1
    zero = jnp.zeros((ROWS, LANES), F32)
    one = jnp.ones((ROWS, LANES), F32)

    def active_at(k):
        return jnp.where(depth > k.astype(F32), 1.0, 0.0)

    def forward(k, carry):
        active, gone, ratio, *before = carry
        below = active_at(k + 1)
        u, v, mix = face_ref[0, k], face_ref[1, k], face_ref[2, k]
        u = jnp.where(inner_east, u * active * pltpu.roll(active, ROWS - 1, 0), 0.0)
        v = jnp.where(inner_north, v * active * pltpu.roll(active, LANES - 1, 1), 0.0)
        up, um = jnp.maximum(u, 0.0), jnp.minimum(u, 0.0)
        vp, vm = jnp.maximum(v, 0.0), jnp.minimum(v, 0.0)
        west, south = pltpu.roll(up, 1, 0), pltpu.roll(vp, 1, 1)
        own = (one - up + pltpu.roll(um, 1, 0)) + (pltpu.roll(vm, 1, 1) - vp)
        down = jnp.where(k < levels - 1, mix * active * below, 0.0)
        inverse = 1.0 / (1.0 + gone + down + gone * ratio)
        new_ratio = -down * inverse
        ratio_ref[k] = new_ratio
        after = []
        for t in range(groups):
            c = c_ref[t, k]
            for _ in range(ADVECT):
                c = (
                    own * c
                    + west * pltpu.roll(c, 1, 0)
                    - um * pltpu.roll(c, ROWS - 1, 0)
                    + south * pltpu.roll(c, 1, 1)
                    - vm * pltpu.roll(c, LANES - 1, 1)
                )
            p = (c + gone * before[t]) * inverse
            x_ref[pl.ds(pl.multiple_of((k * groups + t) * ROWS, ROWS), ROWS), :] = p
            after.append(p)
        return (below, down, new_ratio, *after)

    start = (active_at(jnp.int32(0)), zero, zero, *([zero] * groups))
    lax.fori_loop(0, levels, forward, start)

    def at(k, t):
        return pl.ds(pl.multiple_of((k * groups + t) * ROWS, ROWS), ROWS)

    def back_low(n, x):
        k = levels - 1 - n
        ratio = ratio_ref[k]
        new = []
        for t in range(groups):
            value = x_ref[at(k, t), :] - ratio * x[t]
            x_ref[at(k, t), :] = value
            new.append(value)
        return tuple(new)

    side = side_ref[...]
    deep_depth = jnp.where(side > 0.5, depth, 0.0)
    shallow_depth = jnp.where(side < -0.5, depth, 0.0)

    def back_high(n, x):
        k = half - 1 - n
        other = levels - 1 - k
        ratio = ratio_ref[k]
        low, high = k.astype(F32), other.astype(F32)
        deep_low, deep_high = deep_depth > low, deep_depth > high
        shallow_low, shallow_high = shallow_depth > low, shallow_depth > high
        new = []
        for t in range(groups):
            value = x_ref[at(k, t), :] - ratio * x[t]
            under = x_ref[at(other, t), :]
            new.append(value)
            x_ref[at(k, t), :] = jnp.where(deep_low, value, jnp.where(shallow_high, under, 0.0))
            x_ref[at(other, t), :] = jnp.where(deep_high, under, jnp.where(shallow_low, value, 0.0))
        return tuple(new)

    x = lax.fori_loop(0, half, back_low, tuple([zero] * groups))
    lax.fori_loop(0, half, back_high, x)

    width = fold_ref.shape[0]
    step = 4
    rows = step * groups
    left = iota((rows, LANES), 1) < LANES // 2

    def folded(k):
        parts = []
        for i in range(width):
            first = pl.multiple_of(k * groups * ROWS, ROWS) + HALO + i
            parts.append(x_ref[pl.ds(first, rows, stride=ROWS), :])
        whole = jnp.concatenate(parts, axis=1)
        onehot = jnp.concatenate([fold_ref[i] for i in range(width)], axis=0)
        return picked(whole, onehot)

    def send(n, _):
        k = n * step
        upper, lower = folded(k), folded(k + half)
        here = pl.ds(pl.multiple_of(k * groups, rows), rows)
        for v in range(upper.shape[1] // LANES):
            u = upper[:, v * LANES : (v + 1) * LANES]
            w = lower[:, v * LANES : (v + 1) * LANES]
            out_ref[2 * v, here, :] = jnp.where(left, u, pltpu.roll(w, LANES // 2, 1))
            out_ref[2 * v + 1, here, :] = jnp.where(left, pltpu.roll(u, LANES // 2, 1), w)
        return 0

    lax.fori_loop(0, half // step, send, 0)


def reaction_kernel(
    x_ref, lane_ref, matrix_ref, decay_ref, photic_ref, out_ref, state_ref, light_ref, chl_ref
):
    peers, rows, _ = x_ref.shape
    groups = matrix_ref.shape[0] // (2 * peers)
    half = rows // groups
    quarter = half // 2
    pad = light_ref.shape[0]
    chl_ref[...] = jnp.zeros_like(chl_ref)
    for k in range(half):
        chl_ref[k : k + 1, :] = x_ref[0, k * groups : k * groups + 1, :]
    attenuation = jnp.where(iota((pad, LANES), 0) < half, 0.05 + 0.1 * chl_ref[...], 0.0)
    before = jnp.where(iota((pad, pad), 1) < iota((pad, pad), 0), 1.0, 0.0).astype(F32)
    beyond = jnp.where(iota((pad, pad), 1) > iota((pad, pad), 0), 1.0, 0.0).astype(F32)
    above = jnp.dot(before, attenuation, precision=lax.Precision.HIGHEST, preferred_element_type=F32)
    under = jnp.dot(beyond, attenuation, precision=lax.Precision.HIGHEST, preferred_element_type=F32)
    total = jnp.broadcast_to(jnp.sum(attenuation, axis=0, keepdims=True), (pad, LANES))
    total = pltpu.roll(total, LANES // 2, 1)
    right = iota((pad, LANES), 1) >= LANES // 2
    above = above + jnp.where(right, total, 0.0)
    under = under + jnp.where(right, 0.0, total)
    level = (iota((pad, LANES), 0) + jnp.where(right, half, 0)).astype(F32)
    deep = level < lane_ref[0:1, :]
    light = jnp.exp(-jnp.where(deep, above, under))
    light_ref[...] = light
    heat = HEAT_GAIN * light * (1.0 - jnp.exp(-attenuation))
    chl_ref[...] = heat
    first, second = chl_ref[0:quarter, :], chl_ref[quarter : 2 * quarter, :]
    left = iota((quarter, LANES), 1) < LANES // 2
    outer, inner = jnp.where(left, first, second), jnp.where(left, second, first)
    for q in range(peers):
        out_ref[q, rows:, :] = jnp.zeros((out_ref.shape[1] - rows, LANES), F32)
        out_ref[q, rows : rows + quarter, :] = outer if q in (0, peers - 1) else inner

    span = 2 * groups
    decay = decay_ref[...]
    matrix = matrix_ref[...]
    hi = matrix.astype(BF16)
    low = (matrix - hi.astype(F32)).astype(BF16)
    both = jnp.concatenate([hi, hi], axis=1)
    photic_even, photic_odd = photic_ref[0], photic_ref[1]

    def run(pairs):
        state, push = [], []
        for m in pairs:
            state.append(
                jnp.concatenate([x_ref[s, m * span : (m + 1) * span, :] for s in range(peers)], axis=0)
            )
            push.append(
                photic_even * light_ref[2 * m : 2 * m + 1, :]
                + photic_odd * light_ref[2 * m + 1 : 2 * m + 2, :]
            )
        state, push = jnp.concatenate(state, axis=1), jnp.concatenate(push, axis=1)
        rate = jnp.concatenate([decay] * len(pairs), axis=1)
        for _ in range(SUBSTEPS):
            upper = state.astype(BF16)
            lower = (state - upper.astype(F32)).astype(BF16)
            forcing = (
                jnp.dot(both, jnp.concatenate([upper, lower], axis=0), preferred_element_type=F32)
                + jnp.dot(low, upper, preferred_element_type=F32)
                + push
            )
            state = state * rate + RATE_STEP * jnp.tanh(forcing)
        for n, m in enumerate(pairs):
            for s in range(peers):
                out_ref[s, m * span : (m + 1) * span, :] = state[
                    s * span : (s + 1) * span, n * LANES : (n + 1) * LANES
                ]

    for m in range(0, half // 2, 2):
        run((m, m + 1))


def return_kernel(
    x_ref, c_ref, thermal_ref, depth_ref, side_ref, unfold_ref, place_ref, out_ref, heat_ref, y_ref, h_ref
):
    groups, levels, width, _ = c_ref.shape
    share = thermal_ref.shape[0]
    half = levels // 2
    step = 4
    rows = step * groups
    left = iota((rows, LANES), 1) < LANES // 2
    unfold = unfold_ref[...]

    def spread(k, value):
        whole = picked(value, unfold)
        for i in range(width):
            first = pl.multiple_of(k * groups * ROWS, ROWS) + i
            y_ref[pl.ds(first, rows, stride=ROWS), :] = whole[:, i * LANES : (i + 1) * LANES]

    def open_up(n, _):
        k = n * step
        here = pl.ds(pl.multiple_of(k * groups, rows), rows)
        upper, lower = [], []
        for v in range(x_ref.shape[0] // 2):
            p, q = x_ref[2 * v, here, :], x_ref[2 * v + 1, here, :]
            upper.append(jnp.where(left, p, pltpu.roll(q, LANES // 2, 1)))
            lower.append(jnp.where(left, pltpu.roll(p, LANES // 2, 1), q))
        spread(k, jnp.concatenate(upper, axis=1))
        spread(k + half, jnp.concatenate(lower, axis=1))
        return 0

    lax.fori_loop(0, half // step, open_up, 0)

    depth = depth_ref[...]
    side = side_ref[...]
    deep_depth = jnp.where(side > 0.5, depth, 0.0)
    shallow_depth = jnp.where(side < -0.5, depth, 0.0)

    def merge(k, _):
        other = levels - 1 - k
        deep = deep_depth > k.astype(F32)
        shallow = shallow_depth > k.astype(F32)
        for t in range(groups):
            one = y_ref[pl.ds(pl.multiple_of((k * groups + t) * ROWS, ROWS), width), :]
            two = y_ref[pl.ds(pl.multiple_of((other * groups + t) * ROWS, ROWS), width), :]
            out_ref[t, k] = jnp.where(deep, one, jnp.where(shallow, two, c_ref[t, k]))
        return 0

    lax.fori_loop(0, levels, merge, 0)

    place = place_ref[0]
    begin = groups * half
    halves = ([], [])
    left = iota((share, LANES), 1) < LANES // 2
    for v in range(x_ref.shape[0] // 2):
        p, q = (x_ref[2 * v + n, begin : begin + share, :] for n in (0, 1))
        halves[0].append(jnp.where(left, p, pltpu.roll(q, LANES // 2, 1)))
        halves[1].append(jnp.where(left, pltpu.roll(p, LANES // 2, 1), q))
    first, second = (jnp.concatenate(h, axis=1) for h in halves)
    upper_half = place < 2
    deep_heat = jnp.where(upper_half, first, second)
    shallow_heat = jnp.where(upper_half, second, first)
    flip = jnp.where(iota((share, share), 0) + iota((share, share), 1) == share - 1, 1.0, 0.0)
    shallow_heat = jnp.dot(
        flip.astype(F32), shallow_heat, precision=lax.Precision.HIGHEST, preferred_element_type=F32
    )
    for n, part in enumerate((deep_heat, shallow_heat)):
        whole = picked(part, unfold)
        for i in range(width):
            h_ref[n, pl.ds(i, share, stride=ROWS), :] = whole[:, i * LANES : (i + 1) * LANES]
    for k in range(share):
        level = (place * share + k).astype(F32)
        one, two = h_ref[0, k * ROWS : k * ROWS + width, :], h_ref[1, k * ROWS : k * ROWS + width, :]
        warm = jnp.where(deep_depth > level, one, jnp.where(shallow_depth > level, two, 0.0))
        heat_ref[k] = thermal_ref[k] + warm


def ring(axis):
    count = lax.axis_size(axis)
    forward = [(i, i + 1) for i in range(count - 1)]
    return forward, [(b, a) for a, b in forward]


def edges(block, dim):
    forward, backward = ring("tile")
    size = block.shape[dim]
    low = lax.ppermute(lax.slice_in_dim(block, size - HALO, size, axis=dim), "tile", forward)
    high = lax.ppermute(lax.slice_in_dim(block, 0, HALO, axis=dim), "tile", backward)
    return low, high


def body(
    species_concentration,
    courant_face_numbers,
    diffusive_interface_factor,
    thermal_anomaly_field,
    seawater_indicator,
    wet_layer_number,
    species_coupling_matrix,
    species_photic_factor,
    species_loss_factor,
):
    groups, levels, width, _ = species_concentration.shape
    share = diffusive_interface_factor.shape[0]
    peers = lax.axis_size("comp")
    half = levels // 2
    columns = width * LANES
    lanes = columns // 2
    place = lax.axis_index("comp")
    sds = jax.ShapeDtypeStruct

    depth = jnp.where(seawater_indicator > 0, wet_layer_number, 0).astype(F32)
    flat = jnp.concatenate(
        [species_concentration.reshape(groups * levels, width, LANES), depth[None]], axis=0
    )
    c_low, c_high = edges(flat, 1)
    slices = jnp.concatenate([courant_face_numbers, diffusive_interface_factor[None]], axis=0)
    faces = lax.all_gather(slices, "comp", axis=1, tiled=True)
    f_low, f_high = edges(faces[:2], 2)

    fold, unfold, rank, lane_depth = call(
        lambda *refs: pairing_kernel(levels, *refs),
        (
            sds((width, LANES, lanes), BF16),
            sds((lanes, columns), BF16),
            sds((ROWS, LANES), F32),
            sds((ROWS, lanes), F32),
        ),
        ins=[VMEM],
    )(depth)
    rank = rank[:width]
    over = lane_depth[2, 0] > 0.5
    deep = rank < float(lanes)
    split = groups * levels
    own_ext = jnp.concatenate(
        [c_low[:split], species_concentration.reshape(split, width, LANES), c_high[:split]], axis=1
    ).reshape(groups, levels, ROWS, LANES)
    depth_ext = jnp.concatenate([c_low[split], depth, c_high[split]], axis=0)
    gap = jnp.zeros((1, levels, HALO, LANES), F32)
    face_ext = jnp.concatenate(
        [
            jnp.concatenate([f_low, gap], axis=0),
            faces,
            jnp.concatenate([f_high, gap], axis=0),
        ],
        axis=2,
    )

    eye = jnp.eye(2, dtype=F32)
    matrix = species_coupling_matrix.reshape(peers, groups, peers, groups)
    matrix = matrix[:, None, :, :, None, :] * eye[None, :, None, None, :, None]
    matrix = matrix.reshape(peers * 2 * groups, peers * 2 * groups)

    def spreadable(vector):
        v = jnp.broadcast_to(vector.reshape(peers, 1, groups, 1), (peers, 2, groups, LANES))
        return v

    decay = spreadable(1.0 - RATE_STEP * species_loss_factor).reshape(-1, LANES)
    photic = spreadable(species_photic_factor)[None] * eye[:, None, :, None, None]
    photic = photic.reshape(2, -1, LANES)

    def round_trip(current, temperature, side, a, b):
        side_ext = jnp.pad(side, ((HALO, HALO), (0, 0)))
        folded = call(
            transport_kernel,
            sds((peers, half * groups, LANES), F32),
            scratch=[
                pltpu.VMEM((levels * groups * ROWS, LANES), F32),
                pltpu.VMEM((levels, ROWS, LANES), F32),
            ],
            ins=[VMEM] * 5,
        )(own_ext, face_ext, depth_ext, side_ext, fold)
        arrived = lax.all_to_all(folded, "comp", split_axis=0, concat_axis=0, tiled=True)
        part = lanes // peers
        mine = lax.dynamic_slice_in_dim(jnp.stack([a, b]), place * part, part, axis=1)
        mine = jnp.pad(jnp.concatenate([mine, mine], axis=1), ((0, ROWS - 2), (0, 0)))
        extra = -(-share // ROWS) * ROWS
        reacted = call(
            reaction_kernel,
            sds((peers, half * groups + extra, LANES), F32),
            scratch=[
                pltpu.VMEM((ROWS, LANES), F32),
                pltpu.VMEM((-(-half // ROWS) * ROWS, LANES), F32),
                pltpu.VMEM((-(-half // ROWS) * ROWS, LANES), F32),
            ],
            ins=[VMEM] * 5,
        )(arrived, mine, matrix, decay, photic)
        returned = lax.all_to_all(reacted, "comp", split_axis=0, concat_axis=0, tiled=True)
        return call(
            return_kernel,
            (
                sds((groups, levels, width, LANES), F32),
                sds((share, width, LANES), F32),
            ),
            scratch=[
                pltpu.VMEM((levels * groups * ROWS, LANES), F32),
                pltpu.VMEM((2, -(-share // ROWS) * ROWS * ROWS, LANES), F32),
            ],
            ins=[VMEM] * 6 + [SMEM],
        )(returned, current, temperature, depth, side, unfold, place[None].astype(jnp.int32))

    a, b = lane_depth[0], lane_depth[1]
    sign = jnp.where(deep, 1.0, -1.0).astype(F32)
    side = jnp.where(over & ~deep, 0.0, sign)
    out, heat = round_trip(
        species_concentration, thermal_anomaly_field, side, a, jnp.where(over, 0.0, b)
    )

    def rest(carry):
        _, current, temperature = carry
        current, temperature = round_trip(
            current, temperature, jnp.where(deep, 0.0, sign), jnp.zeros_like(a), b
        )
        return jnp.zeros((), bool), current, temperature

    _, out, heat = lax.while_loop(lambda carry: carry[0], rest, (over, out, heat))
    return out, heat


def solution(mesh):
    in_specs = (
        P("comp", None, "tile", None),
        P(None, "comp", "tile", None),
        P("comp", "tile", None),
        P("comp", "tile", None),
        P("tile", None),
        P("tile", None),
        P(),
        P(),
        P(),
    )
    out_specs = (P("comp", None, "tile", None), P("comp", "tile", None))
    return jax.shard_map(body, mesh=mesh, in_specs=in_specs, out_specs=out_specs, check_vma=False)
```

time: 220 us -> 163 us (0.74)
  Pallas kernels: 0 us -> 45.8 us
  waiting for transfers between devices: 62 us -> 24.5 us
  blocking collectives: 79.5 us -> 50.6 us
  local copies, waits for them, and re-layouts: 20.7 us -> 5.44 us
  matrix products: 13.4 us -> 0 us
  other arithmetic: 20.7 us -> 9.84 us
  starting transfers between devices: 20.6 us -> 25.1 us
    pallas_call x0 -> x4, Pallas kernels: none -> 45.8 us  [the longest x1 32 us: round_trip(): call(transport_kernel, sds((peers, half * groups, LANES), F32), scratch=[...]
    all_to_all x2 -> x1, waiting for transfers between devices: 56.1 us -> 24.2 us  [round_trip(): lax.all_to_all(folded, 'comp', split_axis=0, concat_axis=0, tiled=True)]
    all_to_all x1, blocking collectives: 47.7 us -> 31.2 us  [round_trip(): lax.all_to_all(reacted, 'comp', split_axis=0, concat_axis=0, tiled=True)]
    dot_general x4 -> x0, matrix products: 13.4 us -> none  [reaction(): jnp.dot(species_coupling_matrix, columns_flat, precision=lax.Precision.HI...]
    all_gather x2 -> x1, blocking collectives: 31.8 us -> 19.4 us  [body(): faces = lax.all_gather(slices, 'comp', axis=1, tiled=True)]
    ppermute x4, starting transfers between devices: 11.5 us -> 21.5 us  [the longest x2 17.4 us: edges(): lax.ppermute(lax.slice_in_dim(block, size - HALO, size, axis=dim), 'tile'...]
    add x10 -> x0, other arithmetic: 6.85 us -> none  [the longest x2 3.55 us: advance(): jnp.maximum(speed_east, 0.0) * conc[:, :, :-1]]
    ppermute x4, waiting for transfers between devices: 5.92 us -> 0.21 us  [the longest x2 0.21 us: edges(): lax.ppermute(lax.slice_in_dim(block, 0, HALO, axis=dim), 'tile', backward)]
  transfers between devices with their start and end apart: 6 -> 5, of which waited for: 4 -> 2; matrix products, arithmetic and copies ran while one was open for 2% -> 3% of each run, Pallas kernels for 0% -> 1%
where the time goes in v1:
time: 163 us
  blocking collectives  50.6 us (31%)
  Pallas kernels  45.8 us (28%)
  starting transfers between devices  25.1 us (15%)
  waiting for transfers between devices  24.5 us (15%)
  other arithmetic  9.84 us (6%)
  local copies, waits for them, and re-layouts  5.44 us (3%)
    pallas_call x1, Pallas kernels, round_trip(): call(transport_kernel, sds((peers, half * groups, LANES), F32), scratch=[...  32 us
    all_to_all x1, blocking collectives, round_trip(): lax.all_to_all(reacted, 'comp', split_axis=0, concat_axis=0, tiled=True)  31.2 us
    all_to_all x1, waiting for transfers between devices, round_trip(): lax.all_to_all(folded, 'comp', split_axis=0, concat_axis=0, tiled=True)  24.2 us
    all_gather x1, blocking collectives, body(): faces = lax.all_gather(slices, 'comp', axis=1, tiled=True)  19.4 us
    ppermute x2, starting transfers between devices, edges(): lax.ppermute(lax.slice_in_dim(block, size - HALO, size, axis=dim), 'tile'...  17.4 us
    pallas_call x1, Pallas kernels, round_trip(): call(return_kernel, (sds((groups, levels, width, LANES), F32), sds((share...  7.34 us
    pallas_call x1, Pallas kernels, round_trip(): call(reaction_kernel, sds((peers, half * groups + extra, LANES), F32), sc...  4.9 us
    concatenate x1, other arithmetic, body(): jnp.concatenate([species_concentration.reshape(groups * levels, width, LA...  4.14 us
  transfers between devices with their start and end apart: 5, of which 2 were waited for; matrix products, arithmetic and copies ran while one was open for 3% of the time, Pallas kernels for 1%

profile of v1, /device:TPU:6, one launch (start us, length us, event | category | flops | bytes accessed | tf_op | source)
XLA Modules:
  0.0 162.8 jit_solution(898186937050647297)
XLA Ops:
  0.6 0.7 select_convert_fusion.refs_0_.depth_ref
  1.3 4.1 %fusion.6 = (f32[1057,2,128]{2,1,0:T(2,128)S(1)}, f32[1057,2,128]{2,1,0:T(2,128)S(1)}) fusion(f32[1056,4,128]{2,1,0:T(4,128)} %bitcast.12, f32[1,4,128]{2,1,0:T(4,128)S(1)} %bitcast.15), kind=kLoop, calls=%fused_computation.12 | loop fusion | flops 541184 | bytes 4329472 | tf_op jit(solution)/shard_map/concatenate | solution.py:398
  5.5 2.2 %collective-permute-start.1 = (f32[1057,2,128]{2,1,0:T(2,128)S(1)}, f32[1057,2,128]{2,1,0:T(2,128)S(1)}, u32[]{:S(2)}, u32[]{:S(2)}) collective-permute-start(f32[1057,2,128]{2,1,0:T(2,128)S(1)} %get-tuple-element.185), channel_id=1, source_target_pairs={{4,0},{8,4},{12,8},{16,12},{20,16},{24,20},{28,24},{32,28},{36,32}... | collective-permute-start | bytes 3247112 | tf_op jit(solution)/shard_map/ppermute | solution.py:373
  7.7 2.2 %collective-permute-start = (f32[1057,2,128]{2,1,0:T(2,128)S(1)}, f32[1057,2,128]{2,1,0:T(2,128)S(1)}, u32[]{:S(2)}, u32[]{:S(2)}) collective-permute-start(f32[1057,2,128]{2,1,0:T(2,128)S(1)} %get-tuple-element.184), channel_id=1, source_target_pairs={{0,4},{4,8},{8,12},{12,16},{16,20},{20,24},{24,28},{28,32},{32,36}... | collective-permute-start | bytes 3247112 | tf_op jit(solution)/shard_map/ppermute | solution.py:372
  9.9 19.4 %all_gather.3 = f32[3,88,4,128]{3,2,1,0:T(4,128)S(1)} all-gather(f32[3,22,4,128]{3,2,1,0:T(4,128)S(1)} %pad_maximum_fusion.2), channel_id=1, replica_groups=mesh['tile'=128,'comp'=4] {'comp'}, dimensions={1}, use_global_device_ids=true | all-gather | bytes 675840 | tf_op jit(solution)/shard_map/all_gather | solution.py:403
  29.3 0.1 fusion.8
  29.4 15.2 %collective-permute-start.2 = (f32[2,88,2,128]{3,2,1,0:T(2,128)S(1)}, f32[2,88,2,128]{3,2,1,0:T(2,128)S(1)}, u32[]{:S(2)}, u32[]{:S(2)}) collective-permute-start(f32[2,88,2,128]{3,2,1,0:T(2,128)S(1)} %get-tuple-element.186), channel_id=1, source_target_pairs={{0,4},{4,8},{8,12},{12,16},{16,20},{20,24},{24,28},{28,32},{32,36}... | collective-permute-start | bytes 540680 | tf_op jit(solution)/shard_map/ppermute | solution.py:372
  44.6 1.9 %collective-permute-start.3 = (f32[2,88,2,128]{3,2,1,0:T(2,128)S(1)}, f32[2,88,2,128]{3,2,1,0:T(2,128)S(1)}, u32[]{:S(2)}, u32[]{:S(2)}) collective-permute-start(f32[2,88,2,128]{3,2,1,0:T(2,128)S(1)} %get-tuple-element.187), channel_id=1, source_target_pairs={{4,0},{8,4},{12,8},{16,12},{20,16},{24,20},{28,24},{32,28},{36,32}... | collective-permute-start | bytes 540680 | tf_op jit(solution)/shard_map/ppermute | solution.py:373
  46.6 1.5 shard_map.104
  48.1 0.5 slice.39
  49.3 0.2 collective-permute-done.3
  49.5 0.3 select_maximum_fusion.1.face_ref
  49.9 0.1 slice.53
  50.2 1.7 %copy-done = f32[12,88,4,128]{3,2,1,0:T(4,128)S(1)} copy-done((f32[12,88,4,128]{3,2,1,0:T(4,128)S(1)}, f32[12,88,4,128]{3,2,1,0:T(4,128)}, u32[]{:S(2)}) %copy-start) | copy-done | bytes 2162712
  51.9 3.4 %pad_maximum_fusion.c_ref = f32[12,88,8,128]{3,2,1,0:T(8,128)} fusion(f32[12,88,2,128]{3,2,1,0:T(2,128)S(1)} %bitcast.14, f32[12,88,4,128]{3,2,1,0:T(4,128)S(1)} %copy-done, f32[12,88,2,128]{3,2,1,0:T(2,128)S(1)} %bitcast.13), kind=kLoop, calls=%fused_computation.9 | loop fusion | flops 2162688 | bytes 8650752 | tf_op jit(solution)/shard_map/concatenate | solution.py:420
  55.3 32.0 %shard_map.105 = f32[4,528,128]{2,1,0:T(8,128)} custom-call(f32[12,88,8,128]{3,2,1,0:T(8,128)} %pad_maximum_fusion.c_ref, f32[3,88,8,128]{3,2,1,0:T(8,128)S(1)} %select_maximum_fusion.1.face_ref, f32[8,128]{1,0:T(8,128)S(1)} %pad_maximum_fusion.3.depth_ref, f32[8,128]{1,0:T(8,128)S(1)} %pad.19.side_ref, bf16[4,128,256]{2,1,0:T(8,128)(2,1)S(1)} %get-tuple-element.217.fold_ref), custom_call_target="tpu_custom_call" | custom-call | tf_op jit(solution)/shard_map/pallas_call | solution.py:449
  87.3 3.7 %all-to-all-start.2 = ((f32[4,528,128]{2,1,0:T(8,128)}), f32[4,528,128]{2,1,0:T(8,128)S(1)}, u32[]{:S(2)}, u32[]{:S(2)}) async-start(f32[4,528,128]{2,1,0:T(8,128)} %shard_map.105), calls=%async_computation.2 | async-start | bytes 2162688 | tf_op jit(solution)/shard_map/all_to_all | solution.py:458
  91.5 0.9 broadcast_multiply_fusion.2
  92.4 1.5 mul.49.matrix_ref
  94.3 24.2 %all-to-all-done.2.x_ref = f32[4,528,128]{2,1,0:T(8,128)S(1)} async-done(((f32[4,528,128]{2,1,0:T(8,128)}), f32[4,528,128]{2,1,0:T(8,128)S(1)}, u32[]{:S(2)}, u32[]{:S(2)}) %all-to-all-start.2) | async-done | bytes 1081376 | tf_op jit(solution)/shard_map/all_to_all | solution.py:458
  118.6 4.9 %shard_map.106 = f32[4,552,128]{2,1,0:T(8,128)S(1)} custom-call(f32[4,528,128]{2,1,0:T(8,128)S(1)} %all-to-all-done.2.x_ref, f32[8,128]{1,0:T(8,128)S(1)} %select_maximum_fusion.3.lane_ref, f32[96,96]{1,0:T(8,128)S(1)} %mul.49.matrix_ref, f32[96,128]{1,0:T(8,128)S(1)} %broadcast_in_dim.57.decay_ref, f32[2,96,128]{2,1,0:T(8,128)S(1)} %broadcast_multiply_fusion.3.photic_ref), custom_call_target="tpu_custom_call" | custom-call | tf_op jit(solution)/shard_map/pallas_call | solution.py:463
  123.6 31.2 %all_to_all.20.x_ref = f32[4,552,128]{2,1,0:T(8,128)S(1)} all-to-all(f32[4,552,128]{2,1,0:T(8,128)S(1)} %shard_map.106), channel_id=1, replica_groups=mesh['tile'=128,'comp'=4] {'comp'}, dimensions={0} | all-to-all | bytes 2260992 | tf_op jit(solution)/shard_map/all_to_all | solution.py:473
  154.8 7.3 %shard_map.107 = (f32[12,88,4,128]{3,2,1,0:T(4,128)}, f32[22,4,128]{2,1,0:T(4,128)S(1)}) custom-call(f32[4,552,128]{2,1,0:T(8,128)S(1)} %all_to_all.20.x_ref, f32[12,88,4,128]{3,2,1,0:T(4,128)S(1)} %copy-done, f32[22,4,128]{2,1,0:T(4,128)S(1)} %copy-done.1, f32[4,128]{1,0:T(4,128)S(1)} %select_convert_fusion.refs_0_.depth_ref, ...), custom_call_target="tpu_custom_call" | custom-call | tf_op jit(solution)/shard_map/pallas_call | solution.py:474
  162.2 0.6 copy-done.10
  (52 shorter events, 1.2 us)
Async XLA Ops:
  1.3 8.5 %copy-start.11 = (f32[2,22,4,128]{3,2,1,0:T(4,128)S(1)}, f32[2,22,4,128]{3,2,1,0:T(4,128)}, u32[]{:S(2)}) copy-start(f32[2,22,4,128]{3,2,1,0:T(4,128)} %param.12) | copy-start | bytes 270340
  1.3 8.5 %copy-start.12 = (f32[22,4,128]{2,1,0:T(4,128)S(1)}, f32[22,4,128]{2,1,0:T(4,128)}, u32[]{:S(2)}) copy-start(f32[22,4,128]{2,1,0:T(4,128)} %param.13) | copy-start | bytes 135172
  5.5 44.4 %collective-permute-start.1 = (f32[1057,2,128]{2,1,0:T(2,128)S(1)}, f32[1057,2,128]{2,1,0:T(2,128)S(1)}, u32[]{:S(2)}, u32[]{:S(2)}) collective-permute-start(f32[1057,2,128]{2,1,0:T(2,128)S(1)} %get-tuple-element.185), channel_id=1, source_target_pairs={{4,0},{8,4},{12,8},{16,12},{20,16},{24,20},{28,24},{32,28},{36,32}... | collective-permute-start | bytes 3247112 | tf_op jit(solution)/shard_map/ppermute | solution.py:373
  7.7 42.2 %collective-permute-start = (f32[1057,2,128]{2,1,0:T(2,128)S(1)}, f32[1057,2,128]{2,1,0:T(2,128)S(1)}, u32[]{:S(2)}, u32[]{:S(2)}) collective-permute-start(f32[1057,2,128]{2,1,0:T(2,128)S(1)} %get-tuple-element.184), channel_id=1, source_target_pairs={{0,4},{4,8},{8,12},{12,16},{16,20},{20,24},{24,28},{28,32},{32,36}... | collective-permute-start | bytes 3247112 | tf_op jit(solution)/shard_map/ppermute | solution.py:372
  29.4 19.9 %collective-permute-start.2 = (f32[2,88,2,128]{3,2,1,0:T(2,128)S(1)}, f32[2,88,2,128]{3,2,1,0:T(2,128)S(1)}, u32[]{:S(2)}, u32[]{:S(2)}) collective-permute-start(f32[2,88,2,128]{3,2,1,0:T(2,128)S(1)} %get-tuple-element.186), channel_id=1, source_target_pairs={{0,4},{4,8},{8,12},{12,16},{16,20},{20,24},{24,28},{28,32},{32,36}... | collective-permute-start | bytes 540680 | tf_op jit(solution)/shard_map/ppermute | solution.py:372
  44.6 4.9 %collective-permute-start.3 = (f32[2,88,2,128]{3,2,1,0:T(2,128)S(1)}, f32[2,88,2,128]{3,2,1,0:T(2,128)S(1)}, u32[]{:S(2)}, u32[]{:S(2)}) collective-permute-start(f32[2,88,2,128]{3,2,1,0:T(2,128)S(1)} %get-tuple-element.187), channel_id=1, source_target_pairs={{4,0},{8,4},{12,8},{16,12},{20,16},{24,20},{28,24},{32,28},{36,32}... | collective-permute-start | bytes 540680 | tf_op jit(solution)/shard_map/ppermute | solution.py:373
  48.1 7.2 %copy-start.5 = (bf16[4,128,256]{2,1,0:T(8,128)(2,1)}, bf16[4,128,256]{2,1,0:T(8,128)(2,1)S(1)}, u32[]{:S(2)}) copy-start(bf16[4,128,256]{2,1,0:T(8,128)(2,1)S(1)} %get-tuple-element.217.fold_ref) | copy-start | bytes 786436
  49.9 5.4 %copy-start.2 = (f32[3,88,8,128]{3,2,1,0:T(8,128)}, f32[3,88,8,128]{3,2,1,0:T(8,128)S(1)}, u32[]{:S(2)}) copy-start(f32[3,88,8,128]{3,2,1,0:T(8,128)S(1)} %select_maximum_fusion.1.face_ref) | copy-start | bytes 3244036
  50.1 1.8 %copy-start = (f32[12,88,4,128]{3,2,1,0:T(4,128)S(1)}, f32[12,88,4,128]{3,2,1,0:T(4,128)}, u32[]{:S(2)}) copy-start(f32[12,88,4,128]{3,2,1,0:T(4,128)} %c_ref.1) | copy-start | bytes 6488068
  87.3 3.9 %copy-start.14 = (f32[48]{0:T(128)S(1)}, f32[48]{0:T(128)}, u32[]{:S(2)}) copy-start(f32[48]{0:T(128)} %param.18) | copy-start | bytes 580
  87.3 4.0 %copy-start.13 = (f32[48,48]{1,0:T(8,128)S(1)}, f32[48,48]{1,0:T(8,128)}, u32[]{:S(2)}) copy-start(f32[48,48]{1,0:T(8,128)} %param.17) | copy-start | bytes 27652
  87.3 31.3 %all-to-all-start.2 = ((f32[4,528,128]{2,1,0:T(8,128)}), f32[4,528,128]{2,1,0:T(8,128)S(1)}, u32[]{:S(2)}, u32[]{:S(2)}) async-start(f32[4,528,128]{2,1,0:T(8,128)} %shard_map.105), calls=%async_computation.2 | async-start | bytes 2162688 | tf_op jit(solution)/shard_map/all_to_all | solution.py:458
  91.0 2.9 %copy-start.15 = (f32[48]{0:T(128)S(1)}, f32[48]{0:T(128)}, u32[]{:S(2)}) copy-start(f32[48]{0:T(128)} %param.19) | copy-start | bytes 580
  123.6 31.3 %copy-start.1 = (f32[22,4,128]{2,1,0:T(4,128)S(1)}, f32[22,4,128]{2,1,0:T(4,128)}, u32[]{:S(2)}) copy-start(f32[22,4,128]{2,1,0:T(4,128)} %thermal_ref.1) | copy-start | bytes 135172
  123.6 31.3 %copy-start.8 = (bf16[256,512]{1,0:T(8,128)(2,1)S(1)}, bf16[256,512]{1,0:T(8,128)(2,1)}, u32[]{:S(2)}) copy-start(bf16[256,512]{1,0:T(8,128)(2,1)} %get-tuple-element.221.unfold_ref) | copy-start | bytes 786436
  154.8 7.4 %copy-start.3 = (f32[3,88,8,128]{3,2,1,0:T(8,128)S(1)}, f32[3,88,8,128]{3,2,1,0:T(8,128)}, u32[]{:S(2)}) copy-start(f32[3,88,8,128]{3,2,1,0:T(8,128)} %copy-done.2) | copy-start | bytes 3244036
  154.8 7.4 %copy-start.6 = (bf16[4,128,256]{2,1,0:T(8,128)(2,1)S(1)}, bf16[4,128,256]{2,1,0:T(8,128)(2,1)}, u32[]{:S(2)}) copy-start(bf16[4,128,256]{2,1,0:T(8,128)(2,1)} %copy-done.5) | copy-start | bytes 786436
  162.2 0.6 copy-start.10

commit v2 on v1

--- a/solution.py
+++ b/solution.py
@@ -12,6 +12,7 @@
 LANES = 128
 HALO = 2
 ROWS = 8
+PAD = 16
 F32 = jnp.float32
 BF16 = jnp.bfloat16
 VMEM = pl.BlockSpec(memory_space=pltpu.VMEM)
@@ -42,11 +43,13 @@
 
 
 def picked(x, onehot):
-    total = None
-    for part in split3(x):
-        term = jnp.dot(part, onehot, preferred_element_type=F32)
-        total = term if total is None else total + term
-    return total
+    size = x.shape[0]
+    full = -(-size // PAD) * PAD
+    if full != size:
+        x = jnp.concatenate([x, jnp.zeros((full - size, x.shape[1]), F32)], axis=0)
+    stack = jnp.concatenate(split3(x), axis=0)
+    whole = jnp.dot(stack, onehot, preferred_element_type=F32)
+    return (whole[:size] + whole[full : full + size]) + whole[2 * full : 2 * full + size]
 
 
 def pairing_kernel(levels, depth_ref, fold_ref, unfold_ref, rank_ref, lane_ref):
@@ -95,113 +98,214 @@
     lane_ref[2:3, :] = jnp.broadcast_to(over, (1, lanes))
 
 
-def pack(deep, shallow, x_ref, fold_ref, out_ref, depth, levels, groups):
-    pass
-
-
-def transport_kernel(
-    c_ref, face_ref, depth_ref, side_ref, fold_ref, out_ref, x_ref, ratio_ref
+def split_kernel(c_ref, face_ref, sea_ref, wet_ref, west_a, west_b, east_a, east_b, depth_ref):
+    width = sea_ref.shape[0]
+    half = west_a.shape[1] // PAD
+    levels = 2 * half
+    groups = c_ref.shape[0] // (levels * width)
+    depth = jnp.where(sea_ref[...] > 0, wet_ref[...], 0).astype(F32)
+    depth_ref[...] = depth
+    for part, (west, east) in enumerate(((west_a, east_a), (west_b, east_b))):
+        for i in range(width):
+            side, n = (west, i) if i < HALO else (east, i - HALO)
+            for t in range(groups + 2):
+                ref, g = (c_ref, t) if t < groups else (face_ref, t - groups)
+                first = (g * levels + part * half) * width + i
+                side[n, pl.ds(t, half, stride=PAD), :] = ref[pl.ds(first, half, stride=width), :]
+            side[n, groups + 2 : groups + 3, :] = depth[i : i + 1, :]
+
+
+def factor_kernel(mix_ref, depth_ref, gone_ref, inverse_ref, ratio_ref):
+    width = depth_ref.shape[0]
+    levels = mix_ref.shape[0]
+    depth = depth_ref[...]
+    zero = jnp.zeros_like(depth)
+
+    def step(k, carry):
+        gone, ratio = carry
+        reach = jnp.where(k < levels - 1, (k + 1).astype(F32), 1e9)
+        down = jnp.where(depth > reach, mix_ref[k], 0.0)
+        inverse = 1.0 / (1.0 + gone + down + gone * ratio)
+        ratio = -down * inverse
+        gone_ref[k] = gone
+        inverse_ref[k] = inverse
+        ratio_ref[k] = ratio
+        return down, ratio
+
+    lax.fori_loop(0, levels, step, (zero, zero), unroll=4)
+
+
+def wide(row):
+    return jnp.broadcast_to(row, (ROWS, LANES))
+
+
+def cells_of(west_ref, east_ref, far_west_ref, far_east_ref, groups):
+    columns = [(r, n) for r in (far_west_ref, west_ref, east_ref, far_east_ref) for n in range(HALO)]
+    depth = [r[n, groups + 2 : groups + 3, :] for r, n in columns]
+    return columns, depth
+
+
+def sweep(columns, depth, groups, offset, gone_ref, inverse_ref, x_ref, stencil_ref, before):
+    levels = columns[0][0].shape[1] // PAD
+    cells = len(columns)
+    width = cells - 2 * HALO
+    parts = PAD // ROWS
+
+    number = (iota((levels, LANES), 0) + offset).astype(F32)
+    inner_north = iota((levels, LANES), 1) < LANES - 1
+    active = [jnp.where(number < d, 1.0, 0.0) for d in depth]
+
+    def face(f, e):
+        r, n = columns[e]
+        return r[n, pl.ds(groups + f, levels, stride=PAD), :]
+
+    gain, loss = None, None
+    for e in range(cells - 1):
+        u = face(0, e) * (active[e] * active[e + 1])
+        up, um = jnp.maximum(u, 0.0), jnp.minimum(u, 0.0)
+        if e > 0:
+            v = face(1, e) * active[e] * pltpu.roll(active[e], LANES - 1, 1)
+            v = jnp.where(inner_north, v, 0.0)
+            vp, vm = jnp.maximum(v, 0.0), jnp.minimum(v, 0.0)
+            stencil_ref[e - 1, 0] = (1.0 - up + loss) + (pltpu.roll(vm, 1, 1) - vp)
+            stencil_ref[e - 1, 1] = gain
+            stencil_ref[e - 1, 2] = -um
+            stencil_ref[e - 1, 3] = pltpu.roll(vp, 1, 1)
+            stencil_ref[e - 1, 4] = -vm
+        gain, loss = up, um
+
+    def forward(k, before):
+        after = []
+        for h in range(parts):
+            here = pl.ds(pl.multiple_of(k * PAD, PAD) + h * ROWS, ROWS)
+            there = pl.ds(pl.multiple_of((k + offset) * PAD, PAD) + h * ROWS, ROWS)
+            c = {e: r[n, here, :] for e, (r, n) in enumerate(columns)}
+            for reach in (1, 2):
+                new = {}
+                for e in range(reach, cells - reach):
+                    own, west, east, south, north = (
+                        wide(stencil_ref[e - 1, f, pl.ds(k, 1), :]) for f in range(5)
+                    )
+                    new[e] = (
+                        (own * c[e] + west * c[e - 1])
+                        + east * c[e + 1]
+                        + (south * pltpu.roll(c[e], 1, 1) + north * pltpu.roll(c[e], LANES - 1, 1))
+                    )
+                c = new
+            for i in range(width):
+                gone, inverse = (wide(r[k + offset, i : i + 1, :]) for r in (gone_ref, inverse_ref))
+                p = (c[i + HALO] + gone * before[h * width + i]) * inverse
+                x_ref[there, i * LANES : (i + 1) * LANES] = p
+                after.append(p)
+        return tuple(after)
+
+    return lax.fori_loop(0, levels, forward, before, unroll=2)
+
+
+def zero_rows(count):
+    return tuple([jnp.zeros((ROWS, LANES), F32)] * count)
+
+
+def upper_kernel(
+    west_ref, east_ref, far_west_ref, far_east_ref, gone_ref, inverse_ref, x_ref, stencil_ref
 ):
-    groups, levels = c_ref.shape[:2]
+    width = gone_ref.shape[1]
+    groups = PAD - 4
+    columns, depth = cells_of(west_ref, east_ref, far_west_ref, far_east_ref, groups)
+    zeros = zero_rows(width * PAD // ROWS)
+    sweep(columns, depth, groups, 0, gone_ref, inverse_ref, x_ref, stencil_ref, zeros)
+
+
+def lower_kernel(
+    west_ref,
+    east_ref,
+    far_west_ref,
+    far_east_ref,
+    gone_ref,
+    inverse_ref,
+    ratio_ref,
+    side_ref,
+    fold_ref,
+    begun_ref,
+    out_ref,
+    x_ref,
+    stencil_ref,
+):
+    levels = gone_ref.shape[0]
+    width = gone_ref.shape[1]
+    groups = out_ref.shape[1] * 2 // levels
     half = levels // 2
-    depth = depth_ref[...]
-    row = iota((ROWS, LANES), 0)
-    lane = iota((ROWS, LANES), 1)
-    inner_east = row < ROWS - 1
-    inner_north = lane < LANES - 1
-    zero = jnp.zeros((ROWS, LANES), F32)
-    one = jnp.ones((ROWS, LANES), F32)
-
-    def active_at(k):
-        return jnp.where(depth > k.astype(F32), 1.0, 0.0)
-
-    def forward(k, carry):
-        active, gone, ratio, *before = carry
-        below = active_at(k + 1)
-        u, v, mix = face_ref[0, k], face_ref[1, k], face_ref[2, k]
-        u = jnp.where(inner_east, u * active * pltpu.roll(active, ROWS - 1, 0), 0.0)
-        v = jnp.where(inner_north, v * active * pltpu.roll(active, LANES - 1, 1), 0.0)
-        up, um = jnp.maximum(u, 0.0), jnp.minimum(u, 0.0)
-        vp, vm = jnp.maximum(v, 0.0), jnp.minimum(v, 0.0)
-        west, south = pltpu.roll(up, 1, 0), pltpu.roll(vp, 1, 1)
-        own = (one - up + pltpu.roll(um, 1, 0)) + (pltpu.roll(vm, 1, 1) - vp)
-        down = jnp.where(k < levels - 1, mix * active * below, 0.0)
-        inverse = 1.0 / (1.0 + gone + down + gone * ratio)
-        new_ratio = -down * inverse
-        ratio_ref[k] = new_ratio
-        after = []
-        for t in range(groups):
-            c = c_ref[t, k]
-            for _ in range(ADVECT):
-                c = (
-                    own * c
-                    + west * pltpu.roll(c, 1, 0)
-                    - um * pltpu.roll(c, ROWS - 1, 0)
-                    + south * pltpu.roll(c, 1, 1)
-                    - vm * pltpu.roll(c, LANES - 1, 1)
-                )
-            p = (c + gone * before[t]) * inverse
-            x_ref[pl.ds(pl.multiple_of((k * groups + t) * ROWS, ROWS), ROWS), :] = p
-            after.append(p)
-        return (below, down, new_ratio, *after)
-
-    start = (active_at(jnp.int32(0)), zero, zero, *([zero] * groups))
-    lax.fori_loop(0, levels, forward, start)
-
-    def at(k, t):
-        return pl.ds(pl.multiple_of((k * groups + t) * ROWS, ROWS), ROWS)
+    parts = PAD // ROWS
+    columns, depth = cells_of(west_ref, east_ref, far_west_ref, far_east_ref, groups)
+    last = (half - 1) * PAD
+    before = tuple(
+        begun_ref[last + h * ROWS : last + (h + 1) * ROWS, i * LANES : (i + 1) * LANES]
+        for h in range(parts)
+        for i in range(width)
+    )
+    sweep(columns, depth, groups, half, gone_ref, inverse_ref, x_ref, stencil_ref, before)
+
+    zeros = zero_rows(parts * width)
+
+    def place(k, h, i):
+        return pl.ds(pl.multiple_of(k * PAD, PAD) + h * ROWS, ROWS), pl.ds(i * LANES, LANES)
 
     def back_low(n, x):
         k = levels - 1 - n
-        ratio = ratio_ref[k]
         new = []
-        for t in range(groups):
-            value = x_ref[at(k, t), :] - ratio * x[t]
-            x_ref[at(k, t), :] = value
-            new.append(value)
+        for h in range(parts):
+            for i in range(width):
+                ratio = wide(ratio_ref[k, i : i + 1, :])
+                value = x_ref[place(k, h, i)] - ratio * x[h * width + i]
+                x_ref[place(k, h, i)] = value
+                new.append(value)
         return tuple(new)
 
     side = side_ref[...]
-    deep_depth = jnp.where(side > 0.5, depth, 0.0)
-    shallow_depth = jnp.where(side < -0.5, depth, 0.0)
+    deep_depth, shallow_depth = [], []
+    for i in range(width):
+        kind = side[i : i + 1, :]
+        deep_depth.append(wide(jnp.where(kind > 0.5, depth[i + HALO], 0.0)))
+        shallow_depth.append(wide(jnp.where(kind < -0.5, depth[i + HALO], 0.0)))
 
     def back_high(n, x):
         k = half - 1 - n
         other = levels - 1 - k
-        ratio = ratio_ref[k]
         low, high = k.astype(F32), other.astype(F32)
-        deep_low, deep_high = deep_depth > low, deep_depth > high
-        shallow_low, shallow_high = shallow_depth > low, shallow_depth > high
         new = []
-        for t in range(groups):
-            value = x_ref[at(k, t), :] - ratio * x[t]
-            under = x_ref[at(other, t), :]
-            new.append(value)
-            x_ref[at(k, t), :] = jnp.where(deep_low, value, jnp.where(shallow_high, under, 0.0))
-            x_ref[at(other, t), :] = jnp.where(deep_high, under, jnp.where(shallow_low, value, 0.0))
+        for i in range(width):
+            ratio = wide(ratio_ref[k, i : i + 1, :])
+            deep_low, deep_high = deep_depth[i] > low, deep_depth[i] > high
+            shallow_low, shallow_high = shallow_depth[i] > low, shallow_depth[i] > high
+            for h in range(parts):
+                value = begun_ref[place(k, h, i)] - ratio * x[i * parts + h]
+                under = x_ref[place(other, h, i)]
+                new.append(value)
+                x_ref[place(k, h, i)] = jnp.where(deep_low, value, jnp.where(shallow_high, under, 0.0))
+                x_ref[place(other, h, i)] = jnp.where(deep_high, under, jnp.where(shallow_low, value, 0.0))
         return tuple(new)
 
-    x = lax.fori_loop(0, half, back_low, tuple([zero] * groups))
-    lax.fori_loop(0, half, back_high, x)
-
-    width = fold_ref.shape[0]
+    x = lax.fori_loop(0, half, back_low, zeros, unroll=2)
+    x = tuple(x[h * width + i] for i in range(width) for h in range(parts))
+    lax.fori_loop(0, half, back_high, x, unroll=2)
+
     step = 4
-    rows = step * groups
-    left = iota((rows, LANES), 1) < LANES // 2
-
-    def folded(k):
-        parts = []
-        for i in range(width):
-            first = pl.multiple_of(k * groups * ROWS, ROWS) + HALO + i
-            parts.append(x_ref[pl.ds(first, rows, stride=ROWS), :])
-        whole = jnp.concatenate(parts, axis=1)
-        onehot = jnp.concatenate([fold_ref[i] for i in range(width)], axis=0)
-        return picked(whole, onehot)
+    rows = step * PAD
+    left = iota((step * groups, LANES), 1) < LANES // 2
+    onehot = jnp.concatenate([fold_ref[i] for i in range(width)], axis=0)
 
     def send(n, _):
         k = n * step
-        upper, lower = folded(k), folded(k + half)
-        here = pl.ds(pl.multiple_of(k * groups, rows), rows)
+        begin = pl.multiple_of(k * PAD, rows)
+        both = jnp.concatenate(
+            [x_ref[pl.ds(begin, rows), :], x_ref[pl.ds(begin + half * PAD, rows), :]], axis=0
+        )
+        whole = picked(both, onehot)
+        whole = jnp.concatenate(
+            [whole[j * PAD : j * PAD + groups] for j in range(2 * step)], axis=0
+        )
+        upper, lower = whole[: step * groups], whole[step * groups :]
+        here = pl.ds(pl.multiple_of(k * groups, step * groups), step * groups)
         for v in range(upper.shape[1] // LANES):
             u = upper[:, v * LANES : (v + 1) * LANES]
             w = lower[:, v * LANES : (v + 1) * LANES]
@@ -366,14 +470,6 @@
     return forward, [(b, a) for a, b in forward]
 
 
-def edges(block, dim):
-    forward, backward = ring("tile")
-    size = block.shape[dim]
-    low = lax.ppermute(lax.slice_in_dim(block, size - HALO, size, axis=dim), "tile", forward)
-    high = lax.ppermute(lax.slice_in_dim(block, 0, HALO, axis=dim), "tile", backward)
-    return low, high
-
-
 def body(
     species_concentration,
     courant_face_numbers,
@@ -394,14 +490,27 @@
     place = lax.axis_index("comp")
     sds = jax.ShapeDtypeStruct
 
-    depth = jnp.where(seawater_indicator > 0, wet_layer_number, 0).astype(F32)
-    flat = jnp.concatenate(
-        [species_concentration.reshape(groups * levels, width, LANES), depth[None]], axis=0
-    )
-    c_low, c_high = edges(flat, 1)
     slices = jnp.concatenate([courant_face_numbers, diffusive_interface_factor[None]], axis=0)
     faces = lax.all_gather(slices, "comp", axis=1, tiled=True)
-    f_low, f_high = edges(faces[:2], 2)
+    strip = sds((HALO, half * PAD, LANES), F32)
+    west_a, west_b, east_a, east_b, depth = call(
+        split_kernel, (strip, strip, strip, strip, sds((width, LANES), F32)), ins=[VMEM] * 4
+    )(
+        species_concentration.reshape(groups * levels * width, LANES),
+        faces.reshape(-1, LANES),
+        seawater_indicator,
+        wet_layer_number,
+    )
+    onward, backward = ring("tile")
+    far_west_a = lax.ppermute(east_a, "tile", onward)
+    far_east_a = lax.ppermute(west_a, "tile", backward)
+    far_west_b = lax.ppermute(east_b, "tile", onward)
+    far_east_b = lax.ppermute(west_b, "tile", backward)
+    gone, inverse, ratio = call(
+        factor_kernel,
+        tuple(sds((levels, width, LANES), F32) for _ in range(3)),
+        ins=[VMEM] * 2,
+    )(faces[2], depth)
 
     fold, unfold, rank, lane_depth = call(
         lambda *refs: pairing_kernel(levels, *refs),
@@ -416,21 +525,6 @@
     rank = rank[:width]
     over = lane_depth[2, 0] > 0.5
     deep = rank < float(lanes)
-    split = groups * levels
-    own_ext = jnp.concatenate(
-        [c_low[:split], species_concentration.reshape(split, width, LANES), c_high[:split]], axis=1
-    ).reshape(groups, levels, ROWS, LANES)
-    depth_ext = jnp.concatenate([c_low[split], depth, c_high[split]], axis=0)
-    gap = jnp.zeros((1, levels, HALO, LANES), F32)
-    face_ext = jnp.concatenate(
-        [
-            jnp.concatenate([f_low, gap], axis=0),
-            faces,
-            jnp.concatenate([f_high, gap], axis=0),
-        ],
-        axis=2,
-    )
-
     eye = jnp.eye(2, dtype=F32)
     matrix = species_coupling_matrix.reshape(peers, groups, peers, groups)
     matrix = matrix[:, None, :, :, None, :] * eye[None, :, None, None, :, None]
@@ -444,17 +538,18 @@
     photic = spreadable(species_photic_factor)[None] * eye[:, None, :, None, None]
     photic = photic.reshape(2, -1, LANES)
 
+    stencil = pltpu.VMEM((width + 2, 5, half, LANES), F32)
+    begun = call(
+        upper_kernel, sds((half * PAD, columns), F32), scratch=[stencil], ins=[VMEM] * 6
+    )(west_a, east_a, far_west_a, far_east_a, gone, inverse)
+
     def round_trip(current, temperature, side, a, b):
-        side_ext = jnp.pad(side, ((HALO, HALO), (0, 0)))
         folded = call(
-            transport_kernel,
+            lower_kernel,
             sds((peers, half * groups, LANES), F32),
-            scratch=[
-                pltpu.VMEM((levels * groups * ROWS, LANES), F32),
-                pltpu.VMEM((levels, ROWS, LANES), F32),
-            ],
-            ins=[VMEM] * 5,
-        )(own_ext, face_ext, depth_ext, side_ext, fold)
+            scratch=[pltpu.VMEM((levels * PAD, columns), F32), stencil],
+            ins=[VMEM] * 10,
+        )(west_b, east_b, far_west_b, far_east_b, gone, inverse, ratio, side, fold, begun)
         arrived = lax.all_to_all(folded, "comp", split_axis=0, concat_axis=0, tiled=True)
         part = lanes // peers
         mine = lax.dynamic_slice_in_dim(jnp.stack([a, b]), place * part, part, axis=1)

time: 163 us -> 142 us (0.87); the launches traced: 163 us -> 140 us
  blocking collectives: 50.6 us -> 61.7 us
  starting transfers between devices: 25.1 us -> 14.9 us
  Pallas kernels: 45.8 us -> 36.6 us
  other arithmetic: 9.84 us -> 2.3 us
  waiting for transfers between devices: 24.5 us -> 17.5 us
    ppermute x4, starting transfers between devices: 21.5 us -> 11.1 us  [the longest x1 3.64 us: body(): far_east_b = lax.ppermute(west_b, 'tile', backward)]
    all_to_all x1, blocking collectives: 31.2 us -> 41.3 us  [round_trip(): lax.all_to_all(reacted, 'comp', split_axis=0, concat_axis=0, tiled=True)]
    pallas_call x1 -> x4, Pallas kernels: 32 us -> 23.4 us  [the longest x1 13.2 us: round_trip(): call(lower_kernel, sds((peers, half * groups, LANES), F32), scratch=[pltp...]
    concatenate x4 -> x0, other arithmetic: 7.89 us -> none  [the longest x1 4.14 us: body(): jnp.concatenate([species_concentration.reshape(groups * levels, width, LA...]
    all_to_all x1, waiting for transfers between devices: 24.2 us -> 17.1 us  [round_trip(): lax.all_to_all(folded, 'comp', split_axis=0, concat_axis=0, tiled=True)]
  transfers between devices with their start and end apart: 5 -> 5, of which waited for: 2 -> 2; matrix products, arithmetic and copies ran while one was open for 3% -> 3% of each run, Pallas kernels for 1% -> 7%
where the time goes in v2:
time: 142 us; the launch traced here: 140 us
  blocking collectives  61.7 us (43%)
  Pallas kernels  36.6 us (26%)
  waiting for transfers between devices  17.5 us (12%)
  starting transfers between devices  14.9 us (10%)
  local copies, waits for them, and re-layouts  5.33 us (4%)
  other arithmetic  2.3 us (2%)
  between operations  1.42 us (1%)
    all_to_all x1, blocking collectives, round_trip(): lax.all_to_all(reacted, 'comp', split_axis=0, concat_axis=0, tiled=True)  41.3 us
    all_gather x1, blocking collectives, body(): faces = lax.all_gather(slices, 'comp', axis=1, tiled=True)  20.4 us
    all_to_all x1, waiting for transfers between devices, round_trip(): lax.all_to_all(folded, 'comp', split_axis=0, concat_axis=0, tiled=True)  17.1 us
    pallas_call x1, Pallas kernels, round_trip(): call(lower_kernel, sds((peers, half * groups, LANES), F32), scratch=[pltp...  13.2 us
    pallas_call x1, Pallas kernels, round_trip(): call(return_kernel, (sds((groups, levels, width, LANES), F32), sds((share...  6.76 us
    pallas_call x1, Pallas kernels, body(): call(upper_kernel, sds((half * PAD, columns), F32), scratch=[stencil], in...  6.29 us
    pallas_call x1, Pallas kernels, round_trip(): call(reaction_kernel, sds((peers, half * groups + extra, LANES), F32), sc...  4.9 us
    all_to_all x1, starting transfers between devices, round_trip(): lax.all_to_all(folded, 'comp', split_axis=0, concat_axis=0, tiled=True)  3.8 us
  transfers between devices with their start and end apart: 5, of which 2 were waited for; matrix products, arithmetic and copies ran while one was open for 3% of the time, Pallas kernels for 7%

profile of v2, /device:TPU:6, one launch (start us, length us, event | category | flops | bytes accessed | tf_op | source)
XLA Modules:
  0.0 139.7 jit_solution(18172681266263085305)
XLA Ops:
  0.6 0.9 pad_maximum_fusion
  1.6 20.4 %all_gather.3 = f32[3,88,4,128]{3,2,1,0:T(4,128)S(1)} all-gather(f32[3,22,4,128]{3,2,1,0:T(4,128)S(1)} %pad_maximum_fusion), channel_id=1, replica_groups=mesh['tile'=128,'comp'=4] {'comp'}, dimensions={1}, use_global_device_ids=true | all-gather | bytes 675840 | tf_op jit(solution)/shard_map/all_gather | solution.py:494
  21.9 1.6 %copy-done = f32[12,88,4,128]{3,2,1,0:T(4,128)S(1)} copy-done((f32[12,88,4,128]{3,2,1,0:T(4,128)S(1)}, f32[12,88,4,128]{3,2,1,0:T(4,128)}, u32[]{:S(2)}) %copy-start) | copy-done | bytes 2162712
  23.6 0.7 copy-done.3
  24.2 0.7 copy-done.4
  24.9 2.3 %shard_map.104 = (f32[2,704,128]{2,1,0:T(8,128)S(1)}, f32[2,704,128]{2,1,0:T(8,128)}, f32[2,704,128]{2,1,0:T(8,128)S(1)}, f32[2,704,128]{2,1,0:T(8,128)}, f32[4,128]{1,0:T(4,128)S(1)}) custom-call(f32[4224,128]{1,0:T(8,128)S(1)} %bitcast.8, f32[1056,128]{1,0:T(8,128)S(1)} %bitcast.9, s32[4,128]{1,0:T(4,128)S(1)} %copy-done.3, s32[4,128]{1,0:T(4,128)S(1)} %copy-done.4), custom_call_target="tpu_custom_call" | custom-call | tf_op jit(solution)/shard_map/pallas_call | solution.py:496
  27.2 1.9 %collective-permute-start.2 = (f32[2,704,128]{2,1,0:T(8,128)S(1)}, f32[2,704,128]{2,1,0:T(8,128)S(1)}, u32[]{:S(2)}, u32[]{:S(2)}) collective-permute-start(f32[2,704,128]{2,1,0:T(8,128)S(1)} %get-tuple-element.135.east_ref), channel_id=1, source_target_pairs={{0,4},{4,8},{8,12},{12,16},{16,20},{20,24},{24,28},{28,32},{32,36}... | collective-permute-start | bytes 2162696 | tf_op jit(solution)/shard_map/ppermute | solution.py:505
  29.1 3.6 %collective-permute-start.3 = (f32[2,704,128]{2,1,0:T(8,128)S(1)}, f32[2,704,128]{2,1,0:T(8,128)S(1)}, u32[]{:S(2)}, u32[]{:S(2)}) collective-permute-start(f32[2,704,128]{2,1,0:T(8,128)S(1)} %get-tuple-element.134.west_ref), channel_id=1, source_target_pairs={{4,0},{8,4},{12,8},{16,12},{20,16},{24,20},{28,24},{32,28},{36,32}... | collective-permute-start | bytes 2162696 | tf_op jit(solution)/shard_map/ppermute | solution.py:506
  32.8 1.9 %collective-permute-start = (f32[2,704,128]{2,1,0:T(8,128)}, f32[2,704,128]{2,1,0:T(8,128)}, u32[]{:S(2)}, u32[]{:S(2)}) collective-permute-start(f32[2,704,128]{2,1,0:T(8,128)} %get-tuple-element.277.east_ref), channel_id=1, source_target_pairs={{0,4},{4,8},{8,12},{12,16},{16,20},{20,24},{24,28},{28,32},{32,36}... | collective-permute-start | bytes 2162696 | tf_op jit(solution)/shard_map/ppermute | solution.py:507
  34.7 3.6 %collective-permute-start.1 = (f32[2,704,128]{2,1,0:T(8,128)}, f32[2,704,128]{2,1,0:T(8,128)}, u32[]{:S(2)}, u32[]{:S(2)}) collective-permute-start(f32[2,704,128]{2,1,0:T(8,128)} %get-tuple-element.276.west_ref), channel_id=1, source_target_pairs={{4,0},{8,4},{12,8},{16,12},{20,16},{24,20},{28,24},{32,28},{36,32}... | collective-permute-start | bytes 2162696 | tf_op jit(solution)/shard_map/ppermute | solution.py:508
  38.3 1.6 %shard_map.105 = (bf16[4,128,256]{2,1,0:T(8,128)(2,1)}, bf16[256,512]{1,0:T(8,128)(2,1)}, f32[8,128]{1,0:T(8,128)S(1)}, f32[8,256]{1,0:T(8,128)S(1)}) custom-call(f32[4,128]{1,0:T(4,128)S(1)} %get-tuple-element.287.refs_0_.depth_ref), custom_call_target="tpu_custom_call" | custom-call | tf_op jit(solution)/shard_map/pallas_call | solution.py:515
  39.9 1.6 %shard_map.106 = (f32[88,4,128]{2,1,0:T(4,128)S(1)}, f32[88,4,128]{2,1,0:T(4,128)}, f32[88,4,128]{2,1,0:T(4,128)}) custom-call(f32[88,4,128]{2,1,0:T(4,128)S(1)} %slice_bitcast_fusion.mix_ref, f32[4,128]{1,0:T(4,128)S(1)} %get-tuple-element.287.refs_0_.depth_ref), custom_call_target="tpu_custom_call" | custom-call | tf_op jit(solution)/shard_map/pallas_call | solution.py:509
  41.5 0.5 slice.15
  42.7 6.3 %shard_map.107.begun_ref = f32[704,512]{1,0:T(8,128)} custom-call(f32[2,704,128]{2,1,0:T(8,128)S(1)} %get-tuple-element.134.west_ref, f32[2,704,128]{2,1,0:T(8,128)S(1)} %get-tuple-element.135.east_ref, f32[2,704,128]{2,1,0:T(8,128)S(1)} %collective-permute-done.2.far_west_ref, f32[2,704,128]{2,1,0:T(8,128)S(1)} %collective-permute-done.3.far_east_ref, ...), custom_call_target="tpu_custom_call" | custom-call | tf_op jit(solution)/shard_map/pallas_call | solution.py:542
  49.0 0.4 collective-permute-done.1.far_east_ref
  49.4 13.2 %shard_map.108 = f32[4,528,128]{2,1,0:T(8,128)} custom-call(f32[2,704,128]{2,1,0:T(8,128)} %get-tuple-element.276.west_ref, f32[2,704,128]{2,1,0:T(8,128)} %get-tuple-element.277.east_ref, f32[2,704,128]{2,1,0:T(8,128)} %collective-permute-done.far_west_ref, f32[2,704,128]{2,1,0:T(8,128)} %collective-permute-done.1.far_east_ref, ...), custom_call_target="tpu_custom_call" | custom-call | tf_op jit(solution)/shard_map/pallas_call | solution.py:547
  62.6 3.8 %all-to-all-start.2 = ((f32[4,528,128]{2,1,0:T(8,128)}), f32[4,528,128]{2,1,0:T(8,128)S(1)}, u32[]{:S(2)}, u32[]{:S(2)}) async-start(f32[4,528,128]{2,1,0:T(8,128)} %shard_map.108), calls=%async_computation.2 | async-start | bytes 2162688 | tf_op jit(solution)/shard_map/all_to_all | solution.py:553
  66.7 0.8 mul.45
  67.5 1.1 broadcast_multiply_fusion.2
  68.5 0.5 mul.49.matrix_ref
  69.5 17.1 %all-to-all-done.2.x_ref = f32[4,528,128]{2,1,0:T(8,128)S(1)} async-done(((f32[4,528,128]{2,1,0:T(8,128)}), f32[4,528,128]{2,1,0:T(8,128)S(1)}, u32[]{:S(2)}, u32[]{:S(2)}) %all-to-all-start.2) | async-done | bytes 1081376 | tf_op jit(solution)/shard_map/all_to_all | solution.py:553
  86.7 4.9 %shard_map.109 = f32[4,552,128]{2,1,0:T(8,128)S(1)} custom-call(f32[4,528,128]{2,1,0:T(8,128)S(1)} %all-to-all-done.2.x_ref, f32[8,128]{1,0:T(8,128)S(1)} %select_maximum_fusion.1.lane_ref, f32[96,96]{1,0:T(8,128)S(1)} %mul.49.matrix_ref, f32[96,128]{1,0:T(8,128)S(1)} %broadcast_in_dim.50.decay_ref, f32[2,96,128]{2,1,0:T(8,128)S(1)} %broadcast_multiply_fusion.3.photic_ref), custom_call_target="tpu_custom_call" | custom-call | tf_op jit(solution)/shard_map/pallas_call | solution.py:558
  91.6 41.3 %all_to_all.20.x_ref = f32[4,552,128]{2,1,0:T(8,128)S(1)} all-to-all(f32[4,552,128]{2,1,0:T(8,128)S(1)} %shard_map.109), channel_id=1, replica_groups=mesh['tile'=128,'comp'=4] {'comp'}, dimensions={0} | all-to-all | bytes 2260992 | tf_op jit(solution)/shard_map/all_to_all | solution.py:568
  132.9 6.8 %shard_map.110 = (f32[12,88,4,128]{3,2,1,0:T(4,128)}, f32[22,4,128]{2,1,0:T(4,128)}) custom-call(f32[4,552,128]{2,1,0:T(8,128)S(1)} %all_to_all.20.x_ref, f32[12,88,4,128]{3,2,1,0:T(4,128)S(1)} %copy-done.1, f32[22,4,128]{2,1,0:T(4,128)S(1)} %copy-done.2, f32[4,128]{1,0:T(4,128)S(1)} %get-tuple-element.287.refs_0_.depth_ref, ...), custom_call_target="tpu_custom_call" | custom-call | tf_op jit(solution)/shard_map/pallas_call | solution.py:569
  (35 shorter events, 0.9 us)
Async XLA Ops:
  21.9 1.6 %copy-start = (f32[12,88,4,128]{3,2,1,0:T(4,128)S(1)}, f32[12,88,4,128]{3,2,1,0:T(4,128)}, u32[]{:S(2)}) copy-start(f32[12,88,4,128]{3,2,1,0:T(4,128)} %c_ref.1) | copy-start | bytes 6488068
  23.5 0.7 copy-start.3
  24.2 0.7 copy-start.4
  27.2 15.5 %collective-permute-start.2 = (f32[2,704,128]{2,1,0:T(8,128)S(1)}, f32[2,704,128]{2,1,0:T(8,128)S(1)}, u32[]{:S(2)}, u32[]{:S(2)}) collective-permute-start(f32[2,704,128]{2,1,0:T(8,128)S(1)} %get-tuple-element.135.east_ref), channel_id=1, source_target_pairs={{0,4},{4,8},{8,12},{12,16},{16,20},{20,24},{24,28},{28,32},{32,36}... | collective-permute-start | bytes 2162696 | tf_op jit(solution)/shard_map/ppermute | solution.py:505
  29.1 13.6 %collective-permute-start.3 = (f32[2,704,128]{2,1,0:T(8,128)S(1)}, f32[2,704,128]{2,1,0:T(8,128)S(1)}, u32[]{:S(2)}, u32[]{:S(2)}) collective-permute-start(f32[2,704,128]{2,1,0:T(8,128)S(1)} %get-tuple-element.134.west_ref), channel_id=1, source_target_pairs={{4,0},{8,4},{12,8},{16,12},{20,16},{24,20},{28,24},{32,28},{36,32}... | collective-permute-start | bytes 2162696 | tf_op jit(solution)/shard_map/ppermute | solution.py:506
  32.8 16.3 %collective-permute-start = (f32[2,704,128]{2,1,0:T(8,128)}, f32[2,704,128]{2,1,0:T(8,128)}, u32[]{:S(2)}, u32[]{:S(2)}) collective-permute-start(f32[2,704,128]{2,1,0:T(8,128)} %get-tuple-element.277.east_ref), channel_id=1, source_target_pairs={{0,4},{4,8},{8,12},{12,16},{16,20},{20,24},{24,28},{28,32},{32,36}... | collective-permute-start | bytes 2162696 | tf_op jit(solution)/shard_map/ppermute | solution.py:507
  34.7 14.7 %collective-permute-start.1 = (f32[2,704,128]{2,1,0:T(8,128)}, f32[2,704,128]{2,1,0:T(8,128)}, u32[]{:S(2)}, u32[]{:S(2)}) collective-permute-start(f32[2,704,128]{2,1,0:T(8,128)} %get-tuple-element.276.west_ref), channel_id=1, source_target_pairs={{4,0},{8,4},{12,8},{16,12},{20,16},{24,20},{28,24},{32,28},{36,32}... | collective-permute-start | bytes 2162696 | tf_op jit(solution)/shard_map/ppermute | solution.py:508
  62.6 4.0 %copy-start.7 = (f32[48]{0:T(128)S(1)}, f32[48]{0:T(128)}, u32[]{:S(2)}) copy-start(f32[48]{0:T(128)} %param.18) | copy-start | bytes 580
  62.6 4.2 %copy-start.6 = (f32[48,48]{1,0:T(8,128)S(1)}, f32[48,48]{1,0:T(8,128)}, u32[]{:S(2)}) copy-start(f32[48,48]{1,0:T(8,128)} %param.17) | copy-start | bytes 27652
  62.6 6.5 %copy-start.8 = (f32[48]{0:T(128)S(1)}, f32[48]{0:T(128)}, u32[]{:S(2)}) copy-start(f32[48]{0:T(128)} %param.19) | copy-start | bytes 580
  62.6 24.0 %all-to-all-start.2 = ((f32[4,528,128]{2,1,0:T(8,128)}), f32[4,528,128]{2,1,0:T(8,128)S(1)}, u32[]{:S(2)}, u32[]{:S(2)}) async-start(f32[4,528,128]{2,1,0:T(8,128)} %shard_map.108), calls=%async_computation.2 | async-start | bytes 2162688 | tf_op jit(solution)/shard_map/all_to_all | solution.py:553
  91.6 41.4 %copy-start.1 = (f32[12,88,4,128]{3,2,1,0:T(4,128)S(1)}, f32[12,88,4,128]{3,2,1,0:T(4,128)}, u32[]{:S(2)}) copy-start(f32[12,88,4,128]{3,2,1,0:T(4,128)} %c_ref.1) | copy-start | bytes 6488068
  91.6 41.4 %copy-start.2 = (f32[22,4,128]{2,1,0:T(4,128)S(1)}, f32[22,4,128]{2,1,0:T(4,128)}, u32[]{:S(2)}) copy-start(f32[22,4,128]{2,1,0:T(4,128)} %thermal_ref.1) | copy-start | bytes 135172
